TPU v7x, 128 devices: a whole 4x4x4 slice. The times are simulated.
128 devices in a mesh: group: 4 (over x), dev: 32 (over y, z, core).
Axes of the slice: x: 4, y: 4, z: 4, core: 2. Of those that a mesh axis runs over, the one named last changes fastest.
Arguments:
- source: float32 [64, 1024, 256], P('group', 'dev'), may hold values from -6 to 6
- plane_layer: int32 [256], replicated, may hold values from 0 to 7
- layer_permittivity: float32 [8], replicated, may hold values from 1 to 12
- tile_kind: int32 [8, 128], replicated, may hold values from 0 to 15
- kind_fill: float32 [16], replicated, may hold values from 0.5 to 2
Outputs:
- potential: float32 [64, 1024, 256], P('group', 'dev')
- residual: float32 [64, 1024, 256], P('group', 'dev')
All inputs are finite; a program needn't handle non-finite values.
Results may differ from a plain program's by a relative error of at most 0.00015.
Values sent between devices are 32-bit elements; how exact they have to be, the bound alone decides.
A program may use at most 192 MiB of HBM per device.

v0:
```python
import jax
import jax.numpy as jnp
from jax import lax
from jax.sharding import PartitionSpec as P

DEPTH = 5
COARSE_SWEEPS = 24
TILE = 8


omega_damp = 2.0 / 3.0
NEIGHBOUR_SLICES = (
    (slice(2, None), slice(1, -1), slice(1, -1)),
    (slice(0, -2), slice(1, -1), slice(1, -1)),
    (slice(1, -1), slice(2, None), slice(1, -1)),
    (slice(1, -1), slice(0, -2), slice(1, -1)),
    (slice(1, -1), slice(1, -1), slice(2, None)),
    (slice(1, -1), slice(1, -1), slice(0, -2)),
)


def extended(value, sides, width):
    for axis, dim in sides:
        size, length = (lax.axis_size(axis), value.shape[dim])
        up = [(i, (i + 1) % size) for i in range(size - 1)]
        down = [(j, i) for i, j in up]
        last = lax.slice_in_dim(value, length - width, length, axis=dim)
        initial = lax.slice_in_dim(value, 0, width, axis=dim)
        before = lax.ppermute(last, axis, up)
        after = lax.ppermute(initial, axis, down)
        value = jnp.concatenate([before, value, after], axis=dim)
    return value


def padded_z(array_in):
    return jnp.pad(array_in, ((0, 0), (0, 0), (1, 1)))


def pad_xy(array_in, circle_width):
    return jnp.pad(array_in, ((circle_width, circle_width), (circle_width, circle_width), (0, 0)))


def stencil(value_ext, coeff_ext):
    val_pad = padded_z(value_ext)
    coef_pad = padded_z(coeff_ext)
    centre = val_pad[1:-1, 1:-1, 1:-1]
    coeff_mid = coef_pad[1:-1, 1:-1, 1:-1]
    accum = jnp.zeros_like(centre)
    for where_at in NEIGHBOUR_SLICES:
        accum = accum + (coeff_mid + coef_pad[where_at]) * (centre - val_pad[where_at])
    return 0.5 * accum


def diagonal(coeff_ext):
    coef_pad = padded_z(coeff_ext)
    accum = 6.0 * coef_pad[1:-1, 1:-1, 1:-1]
    for where_at in NEIGHBOUR_SLICES:
        accum = accum + coef_pad[where_at]
    return 0.5 * accum


def relax(value_ext, coeff_ext, source_now, diag_vals, level_scale):
    centre = value_ext[1:-1, 1:-1]
    return (
        centre + omega_damp * (source_now - level_scale * stencil(value_ext, coeff_ext)) / diag_vals
    )


def restrict(array_in):
    size_x, size_y, size_z = array_in.shape
    return (
        array_in.reshape(size_x // 2, 2, size_y // 2, 2, size_z // 2, 2).sum(axis=(1, 3, 5)) * 0.125
    )


def prolong(array_in):
    size_x, size_y, size_z = array_in.shape
    spread = jnp.broadcast_to(
        array_in[:, None, :, None, :, None], (size_x, 2, size_y, 2, size_z, 2)
    )
    return spread.reshape(2 * size_x, 2 * size_y, 2 * size_z)


def coarse_fill(fill_level):
    size_x, size_y = fill_level.shape
    return fill_level.reshape(size_x // 2, 2, size_y // 2, 2).sum(axis=(1, 3)) * 0.25


def coarse_permit(permit_level):
    return permit_level.reshape(-1, 2).sum(axis=1) * 0.5


def global_cycle(depth_now, source_now, fill_level, permit_level):
    level_scale = 0.25**depth_now
    coeff_ext = pad_xy(fill_level[:, :, None] * permit_level[None, None, :], 1)
    diag_vals = level_scale * diagonal(coeff_ext)
    iterate = omega_damp * source_now / diag_vals
    if depth_now == DEPTH:

        def sweep_once(step_num, current):
            return relax(pad_xy(current, 1), coeff_ext, source_now, diag_vals, level_scale)

        return lax.fori_loop(0, COARSE_SWEEPS - 1, sweep_once, iterate)
    iterate = relax(pad_xy(iterate, 1), coeff_ext, source_now, diag_vals, level_scale)
    leftover = source_now - level_scale * stencil(pad_xy(iterate, 1), coeff_ext)
    correction = global_cycle(
        depth_now + 1, restrict(leftover), coarse_fill(fill_level), coarse_permit(permit_level)
    )
    iterate = iterate + prolong(correction)
    iterate = relax(pad_xy(iterate, 1), coeff_ext, source_now, diag_vals, level_scale)
    iterate = relax(pad_xy(iterate, 1), coeff_ext, source_now, diag_vals, level_scale)
    return iterate


def rim(iterate):
    return extended(iterate, (("group", 0), ("dev", 1)), 1)


def on_device(source, plane_layer, layer_permittivity, tile_kind, kind_fill):
    x_index = lax.axis_index("group")
    y_index = lax.axis_index("dev")
    layer_ids = jnp.arange(layer_permittivity.shape[0], dtype=jnp.int32)
    permit = jnp.sum(
        jnp.where(plane_layer[:, None] == layer_ids[None, :], layer_permittivity[None, :], 0.0),
        axis=1,
    )
    kind_ids = jnp.arange(kind_fill.shape[0], dtype=jnp.int32)
    tile_values = jnp.sum(
        jnp.where(tile_kind[:, :, None] == kind_ids[None, None, :], kind_fill[None, None, :], 0.0),
        axis=2,
    )
    tiles_x, tiles_y = tile_values.shape
    fill_map = jnp.broadcast_to(
        tile_values[:, None, :, None], (tiles_x, TILE, tiles_y, TILE)
    ).reshape(tiles_x * TILE, tiles_y * TILE)
    replicate_level = 3

    def window(fill_level, circle_width, size_x, size_y):
        padded = jnp.pad(fill_level, circle_width)
        return lax.dynamic_slice(
            padded,
            (x_index * size_x, y_index * size_y),
            (size_x + 2 * circle_width, size_y + 2 * circle_width),
        )

    def cycle(depth_now, source_now, fill_level, permit_level):
        size_x, size_y, size_z = source_now.shape
        if depth_now == replicate_level:
            gathered = lax.all_gather(source_now, "dev", axis=1, tiled=True)
            gathered = lax.all_gather(gathered, "group", axis=0, tiled=True)
            correction = global_cycle(depth_now, gathered, fill_level, permit_level)
            return (
                lax.dynamic_slice(
                    correction, (x_index * size_x, y_index * size_y, 0), (size_x, size_y, size_z)
                ),
                None,
            )
        level_scale = 0.25**depth_now
        coeff_one = window(fill_level, 1, size_x, size_y)[:, :, None] * permit_level[None, None, :]
        diag_vals = level_scale * diagonal(coeff_one)
        iterate = omega_damp * source_now / diag_vals
        iterate = relax(rim(iterate), coeff_one, source_now, diag_vals, level_scale)
        leftover = source_now - level_scale * stencil(rim(iterate), coeff_one)
        correction, unused_coeff = cycle(
            depth_now + 1, restrict(leftover), coarse_fill(fill_level), coarse_permit(permit_level)
        )
        iterate = iterate + prolong(correction)
        iterate = relax(rim(iterate), coeff_one, source_now, diag_vals, level_scale)
        iterate = relax(rim(iterate), coeff_one, source_now, diag_vals, level_scale)
        return (iterate, coeff_one)

    potential, coeff_top = cycle(0, source, fill_map, permit)
    residual = source - 1.0 * stencil(rim(potential), coeff_top)
    return (potential, residual)


def solution(mesh):
    in_specs = (P("group", "dev", None), P(), P(), P(), P())
    out_specs = (P("group", "dev", None), P("group", "dev", None))
    return jax.shard_map(
        on_device, mesh=mesh, in_specs=in_specs, out_specs=out_specs, check_vma=False
    )
```

profile of v0, /device:TPU:22, one launch (start us, length us, event | category | flops | bytes accessed | tf_op | source)
XLA Modules:
  0.0 481.3 jit_solution(18004240974444080615)
XLA Ops:
  1.4 2.6 broadcast_in_dim.46
  4.0 4.0 reshape.108
  10.3 2.7 collective-permute-start
  15.1 3.7 collective-permute-done.1
  18.8 3.8 collective-permute-start.2
  26.4 3.9 broadcast_in_dim.50
  30.9 4.2 fusion.105
  39.2 4.2 collective-permute-done.5
  43.4 4.3 collective-permute-start.6
  57.0 35.6 %reshape.109 = f32[8,2,16,2,128,2]{5,4,3,2,1,0:T(8,128)} reshape(f32[16,32,256]{2,1,0:T(8,128)} %fusion.85) | data formatting | bytes 1048576 | tf_op jit(solution)/shard_map/reshape | solution.py:72
  92.6 12.2 %reduce_sum.142 = f32[8,16,128]{2,1,0:T(8,128)S(1)} reduce(f32[8,2,16,2,128,2]{5,4,3,2,1,0:T(8,128)} %reshape.109, f32[]{:T(128)} %constant.122.clone.1), dimensions={1,3,5}, to_apply=%region_2.3 | reduce | flops 114688 | bytes 589828 | tf_op jit(solution)/shard_map/reduce_sum | solution.py:72
  110.0 3.5 collective-permute-done.9
  114.1 3.5 collective-permute-start.10
  132.8 3.4 collective-permute-done.13
  141.5 4.7 collective-permute-done.15
  148.5 5.5 %reshape.111 = f32[4,2,8,2,64,2]{5,4,3,2,1,0:T(8,128)} reshape(f32[8,16,128]{2,1,0:T(8,128)S(1)} %fusion.251) | data formatting | bytes 131072 | tf_op jit(solution)/shard_map/reshape | solution.py:72
  154.0 2.5 reduce_sum.144
  169.0 4.4 collective-permute-done.19
  177.7 4.2 collective-permute-done.21
  187.9 2.9 collective-permute-done.23
  195.7 23.2 %all_gather.6 = f32[2,128,32]{2,0,1:T(2,128)S(1)} all-gather(f32[2,4,32]{2,0,1:T(2,128)S(1)} %copy.12), channel_id=1, replica_groups=mesh['group'=4,'dev'=32] {'dev'}, dimensions={1}, use_global_device_ids=true | all-gather | bytes 33792 | tf_op jit(solution)/shard_map/all_gather | solution.py:149
  219.6 12.2 %all_gather.7 = f32[8,128,32]{1,2,0:T(8,128)S(1)} all-gather(f32[2,128,32]{1,2,0:T(8,128)} %copy.13), channel_id=1, replica_groups=mesh['group'=4,'dev'=32] {'group'}, dimensions={0}, use_global_device_ids=true | all-gather | bytes 163840 | tf_op jit(solution)/shard_map/all_gather | solution.py:150
  236.3 10.5 %reshape.113 = f32[4,2,64,2,16,2]{3,2,5,4,1,0:T(8,128)} reshape(f32[8,128,32]{1,2,0:T(8,128)} %fusion.148) | data formatting | bytes 262144 | tf_op jit(solution)/shard_map/reshape | solution.py:72
  246.8 4.0 reduce_sum.148
  255.0 2.8 reshape.114
  261.4 24.0 %while.12 = (s32[]{:T(128)}, f32[2,32,8]{1,2,0:T(8,128)S(1)}, f32[2,32,8]{1,2,0:T(8,128)}, f32[2,32,8]{1,2,0:T(8,128)}, f32[2,32,8]{1,2,0:T(8,128)}, /*index=5*/...) while((s32[]{:T(128)}, f32[2,32,8]{1,2,0:T(8,128)S(1)}, ...), condition=%wide.region_15.16_spmd, body=%wide.region_14.15_spmd.sunk | while | flops 12290 | bytes 92785 | solution.py:103
  293.5 3.9 broadcast_in_dim.54
  297.4 7.4 %reshape.116 = f32[8,128,32]{1,2,0:T(8,128)} reshape(f32[4,2,64,2,16,2]{3,2,5,4,1,0:T(8,128)} %broadcast_in_dim.54) | data formatting | bytes 262144 | tf_op jit(solution)/shard_map/reshape | solution.py:81
  313.9 4.2 collective-permute-done.25
  322.5 4.6 collective-permute-done.27
  327.3 3.9 collective-permute-start.28
  332.6 4.2 collective-permute-done.29
  341.1 4.6 collective-permute-done.31
  345.9 2.6 broadcast_in_dim.56
  348.5 4.6 reshape.118
  357.5 4.2 collective-permute-done.33
  366.1 4.6 collective-permute-done.35
  375.2 4.2 collective-permute-done.37
  381.4 2.6 collective-permute-start.39
  384.0 4.4 collective-permute-done.39
  388.8 11.4 %broadcast_in_dim.57 = f32[8,2,16,2,128,2]{5,4,3,2,1,0:T(8,128)} broadcast(f32[8,16,128]{2,1,0:T(8,128)S(1)} %fusion.214), dimensions={0,2,4} | broadcast | bytes 589824 | tf_op jit(solution)/shard_map/broadcast_in_dim | solution.py:78
  400.1 24.6 %reshape.119 = f32[16,32,256]{2,1,0:T(8,128)} reshape(f32[8,2,16,2,128,2]{5,4,3,2,1,0:T(8,128)} %broadcast_in_dim.57) | data formatting | bytes 1048576 | tf_op jit(solution)/shard_map/reshape | solution.py:81
  429.3 4.4 collective-permute-done.41
  438.1 4.8 collective-permute-done.43
  447.7 4.2 collective-permute-done.45
  456.3 4.8 collective-permute-done.47
  465.9 4.2 collective-permute-done.49
  474.5 4.8 collective-permute-done.51
  (397 shorter events, 186.5 us)
Async XLA Ops:
  10.3 4.8 %collective-permute-start = (f32[1,32,256]{2,1,0:T(8,128)S(1)}, f32[1,32,256]{2,1,0:T(8,128)S(1)}, u32[]{:S(2)}, u32[]{:S(2)}) collective-permute-start(f32[1,32,256]{2,1,0:T(8,128)S(1)} %get-tuple-element.162), channel_id=1, source_target_pairs={{32,0},{64,32},{96,64},{33,1},{65,33},{97,65},{34,2},{66,34},{98,6... | collective-permute-start | bytes 98312 | tf_op jit(solution)/shard_map/ppermute | solution.py:30
  13.0 5.8 %collective-permute-start.1 = (f32[1,32,256]{2,1,0:T(8,128)S(1)}, f32[1,32,256]{2,1,0:T(8,128)S(1)}, u32[]{:S(2)}, u32[]{:S(2)}) collective-permute-start(f32[1,32,256]{2,1,0:T(8,128)S(1)} %get-tuple-element.161), channel_id=1, source_target_pairs={{0,32},{32,64},{64,96},{1,33},{33,65},{65,97},{2,34},{34,66},{66,9... | collective-permute-start | bytes 98312 | tf_op jit(solution)/shard_map/ppermute | solution.py:29
  18.8 11.4 %collective-permute-start.2 = (f32[18,1,256]{2,1,0:T(1,128)S(1)}, f32[18,1,256]{2,1,0:T(1,128)S(1)}, u32[]{:S(2)}, u32[]{:S(2)}) collective-permute-start(f32[18,1,256]{2,1,0:T(1,128)S(1)} %get-tuple-element.152), channel_id=1, source_target_pairs={{1,0},{2,1},{3,2},{4,3},{5,4},{6,5},{7,6},{8,7},{9,8},{10,9},{11,1... | collective-permute-start | bytes 55304 | tf_op jit(solution)/shard_map/ppermute | solution.py:30
  22.7 7.5 %collective-permute-start.3 = (f32[18,1,256]{2,1,0:T(1,128)S(1)}, f32[18,1,256]{2,1,0:T(1,128)S(1)}, u32[]{:S(2)}, u32[]{:S(2)}) collective-permute-start(f32[18,1,256]{2,1,0:T(1,128)S(1)} %get-tuple-element.151), channel_id=1, source_target_pairs={{0,1},{1,2},{2,3},{3,4},{4,5},{5,6},{6,7},{7,8},{8,9},{9,10},{10,1... | collective-permute-start | bytes 55304 | tf_op jit(solution)/shard_map/ppermute | solution.py:29
  35.1 4.0 collective-permute-start.4
  37.6 5.8 %collective-permute-start.5 = (f32[1,32,256]{2,1,0:T(8,128)S(1)}, f32[1,32,256]{2,1,0:T(8,128)S(1)}, u32[]{:S(2)}, u32[]{:S(2)}) collective-permute-start(f32[1,32,256]{2,1,0:T(8,128)S(1)} %get-tuple-element.159), channel_id=1, source_target_pairs={{0,32},{32,64},{64,96},{1,33},{33,65},{65,97},{2,34},{34,66},{66,9... | collective-permute-start | bytes 98312 | tf_op jit(solution)/shard_map/ppermute | solution.py:29
  43.4 9.9 %collective-permute-start.6 = (f32[18,1,256]{2,1,0:T(1,128)S(1)}, f32[18,1,256]{2,1,0:T(1,128)S(1)}, u32[]{:S(2)}, u32[]{:S(2)}) collective-permute-start(f32[18,1,256]{2,1,0:T(1,128)S(1)} %get-tuple-element.150), channel_id=1, source_target_pairs={{1,0},{2,1},{3,2},{4,3},{5,4},{6,5},{7,6},{8,7},{9,8},{10,9},{11,1... | collective-permute-start | bytes 55304 | tf_op jit(solution)/shard_map/ppermute | solution.py:30
  47.8 7.2 %collective-permute-start.7 = (f32[18,1,256]{2,1,0:T(1,128)S(1)}, f32[18,1,256]{2,1,0:T(1,128)S(1)}, u32[]{:S(2)}, u32[]{:S(2)}) collective-permute-start(f32[18,1,256]{2,1,0:T(1,128)S(1)} %get-tuple-element.149), channel_id=1, source_target_pairs={{0,1},{1,2},{2,3},{3,4},{4,5},{5,6},{6,7},{7,8},{8,9},{9,10},{10,1... | collective-permute-start | bytes 55304 | tf_op jit(solution)/shard_map/ppermute | solution.py:29
  105.5 4.5 collective-permute-start.8
  107.9 5.5 %collective-permute-start.9 = (f32[1,16,128]{2,1,0:T(8,128)S(1)}, f32[1,16,128]{2,1,0:T(8,128)S(1)}, u32[]{:S(2)}, u32[]{:S(2)}) collective-permute-start(f32[1,16,128]{2,1,0:T(8,128)S(1)} %get-tuple-element.177), channel_id=1, source_target_pairs={{0,32},{32,64},{64,96},{1,33},{33,65},{65,97},{2,34},{34,66},{66,9... | collective-permute-start | bytes 24584 | tf_op jit(solution)/shard_map/ppermute | solution.py:29
  114.1 8.7 %collective-permute-start.10 = (f32[10,1,128]{2,1,0:T(1,128)}, f32[10,1,128]{2,1,0:T(1,128)}, u32[]{:S(2)}, u32[]{:S(2)}) collective-permute-start(f32[10,1,128]{2,1,0:T(1,128)} %get-tuple-element.170), channel_id=1, source_target_pairs={{1,0},{2,1},{3,2},{4,3},{5,4},{6,5},{7,6},{8,7},{9,8},{10,9},{11,1... | collective-permute-start | bytes 15368 | tf_op jit(solution)/shard_map/ppermute | solution.py:30
  117.5 7.4 %collective-permute-start.11 = (f32[10,1,128]{2,1,0:T(1,128)}, f32[10,1,128]{2,1,0:T(1,128)}, u32[]{:S(2)}, u32[]{:S(2)}) collective-permute-start(f32[10,1,128]{2,1,0:T(1,128)} %get-tuple-element.169), channel_id=1, source_target_pairs={{0,1},{1,2},{2,3},{3,4},{4,5},{5,6},{6,7},{7,8},{8,9},{9,10},{10,1... | collective-permute-start | bytes 15368 | tf_op jit(solution)/shard_map/ppermute | solution.py:29
  128.4 4.3 collective-permute-start.12
  130.6 5.5 %collective-permute-start.13 = (f32[1,16,128]{2,1,0:T(8,128)S(1)}, f32[1,16,128]{2,1,0:T(8,128)S(1)}, u32[]{:S(2)}, u32[]{:S(2)}) collective-permute-start(f32[1,16,128]{2,1,0:T(8,128)S(1)} %get-tuple-element.175), channel_id=1, source_target_pairs={{0,32},{32,64},{64,96},{1,33},{33,65},{65,97},{2,34},{34,66},{66,9... | collective-permute-start | bytes 24584 | tf_op jit(solution)/shard_map/ppermute | solution.py:29
  137.0 4.5 collective-permute-start.14
  139.2 7.0 %collective-permute-start.15 = (f32[10,1,128]{2,1,0:T(1,128)S(1)}, f32[10,1,128]{2,1,0:T(1,128)S(1)}, u32[]{:S(2)}, u32[]{:S(2)}) collective-permute-start(f32[10,1,128]{2,1,0:T(1,128)S(1)} %get-tuple-element.167), channel_id=1, source_target_pairs={{0,1},{1,2},{2,3},{3,4},{4,5},{5,6},{6,7},{7,8},{8,9},{9,10},{10,1... | collective-permute-start | bytes 15368 | tf_op jit(solution)/shard_map/ppermute | solution.py:29
  156.7 5.3 %collective-permute-start.16 = (f32[1,8,64]{2,1,0:T(8,128)S(1)}, f32[1,8,64]{2,1,0:T(8,128)S(1)}, u32[]{:S(2)}, u32[]{:S(2)}) collective-permute-start(f32[1,8,64]{2,1,0:T(8,128)S(1)} %get-tuple-element.194), channel_id=1, source_target_pairs={{32,0},{64,32},{96,64},{33,1},{65,33},{97,65},{34,2},{66,34},{98,6... | collective-permute-start | bytes 6152 | tf_op jit(solution)/shard_map/ppermute | solution.py:30
  158.9 5.5 %collective-permute-start.17 = (f32[1,8,64]{2,1,0:T(8,128)S(1)}, f32[1,8,64]{2,1,0:T(8,128)S(1)}, u32[]{:S(2)}, u32[]{:S(2)}) collective-permute-start(f32[1,8,64]{2,1,0:T(8,128)S(1)} %get-tuple-element.193), channel_id=1, source_target_pairs={{0,32},{32,64},{64,96},{1,33},{33,65},{65,97},{2,34},{34,66},{66,9... | collective-permute-start | bytes 6152 | tf_op jit(solution)/shard_map/ppermute | solution.py:29
  164.4 4.6 collective-permute-start.18
  166.3 7.0 %collective-permute-start.19 = (f32[6,1,64]{2,1,0:T(1,128)S(1)}, f32[6,1,64]{2,1,0:T(1,128)S(1)}, u32[]{:S(2)}, u32[]{:S(2)}) collective-permute-start(f32[6,1,64]{2,1,0:T(1,128)S(1)} %get-tuple-element.185), channel_id=1, source_target_pairs={{0,1},{1,2},{2,3},{3,4},{4,5},{5,6},{6,7},{7,8},{8,9},{9,10},{10,1... | collective-permute-start | bytes 4616 | tf_op jit(solution)/shard_map/ppermute | solution.py:29
  174.2 3.5 collective-permute-start.20
  176.4 5.5 %collective-permute-start.21 = (f32[1,8,64]{2,1,0:T(8,128)S(1)}, f32[1,8,64]{2,1,0:T(8,128)S(1)}, u32[]{:S(2)}, u32[]{:S(2)}) collective-permute-start(f32[1,8,64]{2,1,0:T(8,128)S(1)} %get-tuple-element.191), channel_id=1, source_target_pairs={{0,32},{32,64},{64,96},{1,33},{33,65},{65,97},{2,34},{34,66},{66,9... | collective-permute-start | bytes 6152 | tf_op jit(solution)/shard_map/ppermute | solution.py:29
  181.9 6.0 %collective-permute-start.22 = (f32[6,1,64]{2,1,0:T(1,128)S(1)}, f32[6,1,64]{2,1,0:T(1,128)S(1)}, u32[]{:S(2)}, u32[]{:S(2)}) collective-permute-start(f32[6,1,64]{2,1,0:T(1,128)S(1)} %get-tuple-element.184), channel_id=1, source_target_pairs={{1,0},{2,1},{3,2},{4,3},{5,4},{6,5},{7,6},{8,7},{9,8},{10,9},{11,1... | collective-permute-start | bytes 4616 | tf_op jit(solution)/shard_map/ppermute | solution.py:30
  183.8 7.0 %collective-permute-start.23 = (f32[6,1,64]{2,1,0:T(1,128)S(1)}, f32[6,1,64]{2,1,0:T(1,128)S(1)}, u32[]{:S(2)}, u32[]{:S(2)}) collective-permute-start(f32[6,1,64]{2,1,0:T(1,128)S(1)} %get-tuple-element.183), channel_id=1, source_target_pairs={{0,1},{1,2},{2,3},{3,4},{4,5},{5,6},{6,7},{7,8},{8,9},{9,10},{10,1... | collective-permute-start | bytes 4616 | tf_op jit(solution)/shard_map/ppermute | solution.py:29
  312.6 5.5 %collective-permute-start.25 = (f32[1,8,64]{2,1,0:T(8,128)S(1)}, f32[1,8,64]{2,1,0:T(8,128)S(1)}, u32[]{:S(2)}, u32[]{:S(2)}) collective-permute-start(f32[1,8,64]{2,1,0:T(8,128)S(1)} %get-tuple-element.189), channel_id=1, source_target_pairs={{0,32},{32,64},{64,96},{1,33},{33,65},{65,97},{2,34},{34,66},{66,9... | collective-permute-start | bytes 6152 | tf_op jit(solution)/shard_map/ppermute | solution.py:29
  318.1 4.3 collective-permute-start.26
  320.0 7.0 %collective-permute-start.27 = (f32[6,1,64]{2,1,0:T(1,128)S(1)}, f32[6,1,64]{2,1,0:T(1,128)S(1)}, u32[]{:S(2)}, u32[]{:S(2)}) collective-permute-start(f32[6,1,64]{2,1,0:T(1,128)S(1)} %get-tuple-element.181), channel_id=1, source_target_pairs={{0,1},{1,2},{2,3},{3,4},{4,5},{5,6},{6,7},{7,8},{8,9},{9,10},{10,1... | collective-permute-start | bytes 4616 | tf_op jit(solution)/shard_map/ppermute | solution.py:29
  327.3 5.2 %collective-permute-start.28 = (f32[1,8,64]{2,1,0:T(8,128)S(1)}, f32[1,8,64]{2,1,0:T(8,128)S(1)}, u32[]{:S(2)}, u32[]{:S(2)}) collective-permute-start(f32[1,8,64]{2,1,0:T(8,128)S(1)} %get-tuple-element.188), channel_id=1, source_target_pairs={{32,0},{64,32},{96,64},{33,1},{65,33},{97,65},{34,2},{66,34},{98,6... | collective-permute-start | bytes 6152 | tf_op jit(solution)/shard_map/ppermute | solution.py:30
  331.2 5.5 %collective-permute-start.29 = (f32[1,8,64]{2,1,0:T(8,128)S(1)}, f32[1,8,64]{2,1,0:T(8,128)S(1)}, u32[]{:S(2)}, u32[]{:S(2)}) collective-permute-start(f32[1,8,64]{2,1,0:T(8,128)S(1)} %get-tuple-element.187), channel_id=1, source_target_pairs={{0,32},{32,64},{64,96},{1,33},{33,65},{65,97},{2,34},{34,66},{66,9... | collective-permute-start | bytes 6152 | tf_op jit(solution)/shard_map/ppermute | solution.py:29
  336.8 4.3 collective-permute-start.30
  338.7 7.0 %collective-permute-start.31 = (f32[6,1,64]{2,1,0:T(1,128)S(1)}, f32[6,1,64]{2,1,0:T(1,128)S(1)}, u32[]{:S(2)}, u32[]{:S(2)}) collective-permute-start(f32[6,1,64]{2,1,0:T(1,128)S(1)} %get-tuple-element.179), channel_id=1, source_target_pairs={{0,1},{1,2},{2,3},{3,4},{4,5},{5,6},{6,7},{7,8},{8,9},{9,10},{10,1... | collective-permute-start | bytes 4616 | tf_op jit(solution)/shard_map/ppermute | solution.py:29
  356.2 5.5 %collective-permute-start.33 = (f32[1,16,128]{2,1,0:T(8,128)S(1)}, f32[1,16,128]{2,1,0:T(8,128)S(1)}, u32[]{:S(2)}, u32[]{:S(2)}) collective-permute-start(f32[1,16,128]{2,1,0:T(8,128)S(1)} %get-tuple-element.173), channel_id=1, source_target_pairs={{0,32},{32,64},{64,96},{1,33},{33,65},{65,97},{2,34},{34,66},{66,9... | collective-permute-start | bytes 24584 | tf_op jit(solution)/shard_map/ppermute | solution.py:29
  361.7 4.3 collective-permute-start.34
  363.6 7.0 %collective-permute-start.35 = (f32[10,1,128]{2,1,0:T(1,128)S(1)}, f32[10,1,128]{2,1,0:T(1,128)S(1)}, u32[]{:S(2)}, u32[]{:S(2)}) collective-permute-start(f32[10,1,128]{2,1,0:T(1,128)S(1)} %get-tuple-element.165), channel_id=1, source_target_pairs={{0,1},{1,2},{2,3},{3,4},{4,5},{5,6},{6,7},{7,8},{8,9},{9,10},{10,1... | collective-permute-start | bytes 15368 | tf_op jit(solution)/shard_map/ppermute | solution.py:29
  373.9 5.5 %collective-permute-start.37 = (f32[1,16,128]{2,1,0:T(8,128)S(1)}, f32[1,16,128]{2,1,0:T(8,128)S(1)}, u32[]{:S(2)}, u32[]{:S(2)}) collective-permute-start(f32[1,16,128]{2,1,0:T(8,128)S(1)} %get-tuple-element.171), channel_id=1, source_target_pairs={{0,32},{32,64},{64,96},{1,33},{33,65},{65,97},{2,34},{34,66},{66,9... | collective-permute-start | bytes 24584 | tf_op jit(solution)/shard_map/ppermute | solution.py:29
  379.4 4.6 collective-permute-start.38
  381.4 7.0 %collective-permute-start.39 = (f32[10,1,128]{2,1,0:T(1,128)S(1)}, f32[10,1,128]{2,1,0:T(1,128)S(1)}, u32[]{:S(2)}, u32[]{:S(2)}) collective-permute-start(f32[10,1,128]{2,1,0:T(1,128)S(1)} %get-tuple-element.163), channel_id=1, source_target_pairs={{0,1},{1,2},{2,3},{3,4},{4,5},{5,6},{6,7},{7,8},{8,9},{9,10},{10,1... | collective-permute-start | bytes 15368 | tf_op jit(solution)/shard_map/ppermute | solution.py:29
  425.8 3.5 collective-permute-start.40
  427.8 5.9 %collective-permute-start.41 = (f32[1,32,256]{2,1,0:T(8,128)S(1)}, f32[1,32,256]{2,1,0:T(8,128)S(1)}, u32[]{:S(2)}, u32[]{:S(2)}) collective-permute-start(f32[1,32,256]{2,1,0:T(8,128)S(1)} %get-tuple-element.157), channel_id=1, source_target_pairs={{0,32},{32,64},{64,96},{1,33},{33,65},{65,97},{2,34},{34,66},{66,9... | collective-permute-start | bytes 98312 | tf_op jit(solution)/shard_map/ppermute | solution.py:29
  433.8 4.3 collective-permute-start.42
  435.7 7.2 %collective-permute-start.43 = (f32[18,1,256]{2,1,0:T(1,128)S(1)}, f32[18,1,256]{2,1,0:T(1,128)S(1)}, u32[]{:S(2)}, u32[]{:S(2)}) collective-permute-start(f32[18,1,256]{2,1,0:T(1,128)S(1)} %get-tuple-element.147), channel_id=1, source_target_pairs={{0,1},{1,2},{2,3},{3,4},{4,5},{5,6},{6,7},{7,8},{8,9},{9,10},{10,1... | collective-permute-start | bytes 55304 | tf_op jit(solution)/shard_map/ppermute | solution.py:29
  444.2 3.5 collective-permute-start.44
  446.1 5.8 %collective-permute-start.45 = (f32[1,32,256]{2,1,0:T(8,128)S(1)}, f32[1,32,256]{2,1,0:T(8,128)S(1)}, u32[]{:S(2)}, u32[]{:S(2)}) collective-permute-start(f32[1,32,256]{2,1,0:T(8,128)S(1)} %get-tuple-element.155), channel_id=1, source_target_pairs={{0,32},{32,64},{64,96},{1,33},{33,65},{65,97},{2,34},{34,66},{66,9... | collective-permute-start | bytes 98312 | tf_op jit(solution)/shard_map/ppermute | solution.py:29
  452.0 4.3 collective-permute-start.46
  453.9 7.2 %collective-permute-start.47 = (f32[18,1,256]{2,1,0:T(1,128)S(1)}, f32[18,1,256]{2,1,0:T(1,128)S(1)}, u32[]{:S(2)}, u32[]{:S(2)}) collective-permute-start(f32[18,1,256]{2,1,0:T(1,128)S(1)} %get-tuple-element.145), channel_id=1, source_target_pairs={{0,1},{1,2},{2,3},{3,4},{4,5},{5,6},{6,7},{7,8},{8,9},{9,10},{10,1... | collective-permute-start | bytes 55304 | tf_op jit(solution)/shard_map/ppermute | solution.py:29
  464.3 5.8 %collective-permute-start.49 = (f32[1,32,256]{2,1,0:T(8,128)S(1)}, f32[1,32,256]{2,1,0:T(8,128)S(1)}, u32[]{:S(2)}, u32[]{:S(2)}) collective-permute-start(f32[1,32,256]{2,1,0:T(8,128)S(1)} %get-tuple-element.153), channel_id=1, source_target_pairs={{0,32},{32,64},{64,96},{1,33},{33,65},{65,97},{2,34},{34,66},{66,9... | collective-permute-start | bytes 98312 | tf_op jit(solution)/shard_map/ppermute | solution.py:29
  470.1 4.3 collective-permute-start.50
  472.1 7.2 %collective-permute-start.51 = (f32[18,1,256]{2,1,0:T(1,128)S(1)}, f32[18,1,256]{2,1,0:T(1,128)S(1)}, u32[]{:S(2)}, u32[]{:S(2)}) collective-permute-start(f32[18,1,256]{2,1,0:T(1,128)S(1)} %get-tuple-element.143), channel_id=1, source_target_pairs={{0,1},{1,2},{2,3},{3,4},{4,5},{5,6},{6,7},{7,8},{8,9},{9,10},{10,1... | collective-permute-start | bytes 55304 | tf_op jit(solution)/shard_map/ppermute | solution.py:29
  (66 other events, 955.3 us)
where the time goes:
time: 487 us; the launch traced here: 481 us
  local copies, waits for them, and re-layouts  145 us (30%)
  starting transfers between devices  107 us (22%)
  waiting for transfers between devices  100 us (21%)
  other arithmetic  90.2 us (19%)
  blocking collectives  35.4 us (7%)
    ppermute x26, waiting for transfers between devices, extended(): before = lax.ppermute(last, axis, up)  99.3 us
    ppermute x26, starting transfers between devices, extended(): after = lax.ppermute(initial, axis, down)  60.3 us
    reshape x5, local copies, waits for them, and re-layouts, restrict(): array_in.reshape(size_x // 2, 2, size_y // 2, 2, size_z // 2, 2)  56.5 us
    ppermute x26, starting transfers between devices, extended(): before = lax.ppermute(last, axis, up)  46.9 us
    reshape x5, local copies, waits for them, and re-layouts, prolong(): return spread.reshape(2 * size_x, 2 * size_y, 2 * size_z)  40.3 us
    add x38, other arithmetic, relax(): centre + omega_damp * (source_now - level_scale * stencil(value_ext, coef...  38.1 us
    all_gather x1, blocking collectives, cycle(): gathered = lax.all_gather(source_now, 'dev', axis=1, tiled=True)  23.2 us
    reduce_sum x5, other arithmetic, restrict(): array_in.reshape(size_x // 2, 2, size_y // 2, 2, size_z // 2, 2)  21.9 us
  transfers between devices with their start and end apart: 52, of which 29 were waited for; matrix products, arithmetic and copies ran while one was open for 4% of the time, Pallas kernels for 0%

commit v1 on v0

v1 whole, which is shorter than its diff:
```python
import functools

import jax
import jax.numpy as jnp
from jax import lax
from jax.experimental import pallas as pl
from jax.experimental.pallas import tpu as pltpu
from jax.sharding import PartitionSpec as P

MESH = pl.DeviceIdType.MESH
OMEGA = 2.0 / 3.0
KEEP = 1.0 - OMEGA
SWEEPS = 24
NEIGHBOURS = tuple(
    (dx, dy) for dx in (-1, 0, 1) for dy in (-1, 0, 1) if (dx, dy) != (0, 0)
)


def kernel(
    groups,
    devs,
    layers_ref,
    kinds_ref,
    permit_ref,
    fill_ref,
    source,
    pot_ref,
    res_ref,
    F0, V0, W0, B0, INV0, A0, AXP0, AXM0, AYP0, AYM0, RF0, HF0, FX0, T0, P0,
    F1, V1, W1, B1, INV1, A1, AXP1, AXM1, AYP1, AYM1, RF1, HF1, FX1, T1, P1,
    F2, V2, W2, B2, INV2, A2, AXP2, AXM2, AYP2, AYM2, RF2, HF2, FX2, UU,
    FA, G, F4, F5, FC, VC, WC, BC, INVC, AC, AXPC, AXMC, AYPC, AYMC,
    local_sem, s0_send, s0_recv, s0l_send, s0l_recv, s1_send, s1_recv, s1l_send, s1l_recv,
    s2_send, s2_recv, s3_send, s3_recv,
):
    g = lax.axis_index("group")
    d = lax.axis_index("dev")
    f32 = jnp.float32
    lane = lax.broadcasted_iota(jnp.int32, (8, 128), 1)
    sub = lax.broadcasted_iota(jnp.int32, (8, 128), 0)
    even = (lane & 1) == 0

    def peer(dx, dy):
        return (lax.rem(g + dx + groups, groups), lax.rem(d + dy + devs, devs))

    def roll(v, shift):
        return pltpu.roll(v, shift % 128, 1)

    def sroll(v, shift):
        return pltpu.roll(v, shift % 8, 0)

    barrier = pltpu.get_barrier_semaphore()
    group_offsets = tuple(range(1, groups))
    column = [(dx, dy) for dx in range(groups) for dy in (-1, 0, 1) if (dx, dy) != (0, 0)]
    for dx, dy in column:
        pl.semaphore_signal(barrier, inc=1, device_id=peer(dx, dy), device_id_type=MESH)

    def greet(k, carry):
        pl.semaphore_signal(barrier, inc=1, device_id=(g, lax.rem(d + k, devs)), device_id_type=MESH)
        return carry

    lax.fori_loop(2, devs - 1, greet, 0)
    own = [
        pltpu.make_async_copy(
            source.at[:, :, h * 128 : h * 128 + 128], F0.at[h, 4:20, 8:40, :], local_sem.at[h]
        )
        for h in range(2)
    ]
    for copy in own:
        copy.start()
    pl.semaphore_wait(barrier, len(column) + devs - 3)

    def halo0(dx, dy, h, late):
        px = {0: (0, 16, 4), 1: (14, 2, 2), -1: (0, 2, 20)}[dx]
        if late:
            px = {1: (12, 2, 0), -1: (2, 2, 22)}[dx]
        py = {0: (0, 32, 8), 1: (24, 8, 0), -1: (0, 8, 40)}[dy]
        slot = ((dx + 1) * 3 + dy + 1) * 2 + h
        send, recv = (s0l_send, s0l_recv) if late else (s0_send, s0_recv)
        return pltpu.make_async_remote_copy(
            src_ref=source.at[px[0] : px[0] + px[1], py[0] : py[0] + py[1], h * 128 : h * 128 + 128],
            dst_ref=F0.at[h, px[2] : px[2] + px[1], py[2] : py[2] + py[1], :],
            send_sem=send.at[slot],
            recv_sem=recv.at[slot],
            device_id=peer(dx, dy),
            device_id_type=MESH,
        )

    first0 = [halo0(dx, dy, h, False) for dx, dy in NEIGHBOURS for h in range(2)]
    late0 = [halo0(dx, dy, h, True) for dx, dy in NEIGHBOURS if dx for h in range(2)]
    for copy in first0:
        copy.start()

    def halo1(dx, dy, late):
        px = {0: (0, 8, 5), 1: (6, 2, 3), -1: (0, 2, 13)}[dx]
        if late:
            px = {1: (3, 3, 0), -1: (2, 3, 15)}[dx]
        py = {0: (0, 16, 8), 1: (8, 8, 0), -1: (0, 8, 24)}[dy]
        slot = (dx + 1) * 3 + dy + 1
        send, recv = (s1l_send, s1l_recv) if late else (s1_send, s1_recv)
        return pltpu.make_async_remote_copy(
            src_ref=F1.at[px[0] + 5 : px[0] + px[1] + 5, py[0] + 8 : py[0] + py[1] + 8, :],
            dst_ref=F1.at[px[2] : px[2] + px[1], py[2] : py[2] + py[1], :],
            send_sem=send.at[slot],
            recv_sem=recv.at[slot],
            device_id=peer(dx, dy),
            device_id_type=MESH,
        )

    first1 = [halo1(dx, dy, False) for dx, dy in NEIGHBOURS]
    late1 = [halo1(dx, dy, True) for dx, dy in NEIGHBOURS if dx]

    def block2(slot):
        dx, dy = column[slot]
        return pltpu.make_async_remote_copy(
            src_ref=F2.at[pl.ds(4 * g, 4), 8:16, :],
            dst_ref=F2.at[pl.ds(4 * g, 4), 8 - 8 * dy : 16 - 8 * dy, :],
            send_sem=s2_send.at[slot],
            recv_sem=s2_recv.at[slot],
            device_id=peer(dx, dy),
            device_id_type=MESH,
        )

    first2 = [block2(slot) for slot in range(len(column))]

    kinds = kinds_ref[...]
    fills = jnp.zeros((8, 128), f32)
    for kind in range(fill_ref.shape[0]):
        fills = jnp.where(kinds == kind, fill_ref[kind], fills)
    fills = jnp.where(lane < 4 * devs, fills, 0.0)
    shifted = pltpu.roll(fills, lax.rem(8 + 128 - 4 * d + 128, 128), 1)
    tile_y = 4 * d - 8 + lane
    shifted = jnp.where((tile_y >= 0) & (tile_y < 4 * devs), shifted, 0.0)
    zero = jnp.zeros((8, 128), f32)
    for c in range(3):
        for x in (0, 1, 10, 11):
            FA[x, 8 * c : 8 * c + 8, :] = zero
        for x in range(8):
            row = jnp.broadcast_to(shifted[x : x + 1, :], (8, 128))
            picked = jnp.sum(jnp.where(lane == sub + 8 * c, row, 0.0), axis=1, keepdims=True)
            FA[x + 2, 8 * c : 8 * c + 8, :] = jnp.broadcast_to(picked, (8, 128))

    permit0 = []
    for h in range(2):
        layer = jnp.broadcast_to(layers_ref[h : h + 1, :], (8, 128))
        value = jnp.zeros((8, 128), f32)
        for k in range(permit_ref.shape[0]):
            value = jnp.where(layer == k, permit_ref[k], value)
        permit0.append(value)

    def zup0(h0, h1):
        r0, r1 = roll(h0, -1), roll(h1, -1)
        return jnp.where(lane == 127, r1, r0), r1

    def zdn0(h0, h1):
        r0, r1 = roll(h0, 1), roll(h1, 1)
        return r0, jnp.where(lane == 0, r0, r1)

    def zup(v, level):
        step = 1 << level
        return jnp.where(lane >= 128 - step, roll(v, -(step + 1)), roll(v, -step))

    def zdn(v, level):
        step = 1 << level
        return jnp.where(lane < step, roll(v, step + 1), roll(v, step))

    def pair(v, step):
        return v + jnp.where((lane & step) == 0, roll(v, -step), roll(v, step))

    def spair(v, step):
        return v + jnp.where((sub & step) == 0, sroll(v, -step), sroll(v, step))

    def halves(h0, h1):
        return jnp.where(even, h0, h1) + jnp.where(even, roll(h0, -1), roll(h1, 1))

    pu0, pu1 = zup0(*permit0)
    pd0, pd1 = zdn0(*permit0)
    RP0 = [1.0 / p for p in permit0]
    ru = [pu0 * RP0[0], jnp.where(lane == 127, 0.0, pu1 * RP0[1])]
    rd = [jnp.where(lane == 0, 0.0, pd0 * RP0[0]), pd1 * RP0[1]]
    BU0 = [1.0 + ru[0], jnp.where(lane == 127, 0.0, 1.0 + ru[1])]
    BD0 = [jnp.where(lane == 0, 0.0, 1.0 + rd[0]), 1.0 + rd[1]]
    BS0 = [2.0 + ru[h] + rd[h] for h in range(2)]
    permits = [None, 0.5 * halves(*permit0)]
    for level in (2, 3, 4, 5):
        permits.append(0.5 * pair(permits[level - 1], 1 << (level - 1)))
    RPS, BU, BD, BS = [None], [None], [None], [None]
    for level in range(1, 6):
        p = permits[level]
        step = 1 << level
        rp = 1.0 / p
        top = (lane >= 128 - step) & ((lane & 1) == 1)
        bottom = (lane < step) & even
        up = jnp.where(top, 0.0, zup(p, level) * rp)
        dn = jnp.where(bottom, 0.0, zdn(p, level) * rp)
        RPS.append(rp)
        BU.append(jnp.where(top, 0.0, 1.0 + up))
        BD.append(jnp.where(bottom, 0.0, 1.0 + dn))
        BS.append(2.0 + up + dn)

    for t in range(6):
        for j in range(8):
            FX0[t, 8 * j : 8 * j + 8, :] = jnp.broadcast_to(FA[2 * g + t, 6 + j : 7 + j, :], (8, 128))

    def weights0(c, carry):
        at = pl.multiple_of(8 * c, 8)
        out = pl.ds(at, 8)
        for t in range(4):
            f = FX0[t + 1, pl.ds(at + 12, 8), :]
            inside = f > 0.0
            rf = 1.0 / jnp.where(inside, f, 1.0)
            ryp = FX0[t + 1, pl.ds(at + 13, 8), :] * rf
            rym = FX0[t + 1, pl.ds(at + 11, 8), :] * rf
            rxp = FX0[t + 2, pl.ds(at + 12, 8), :] * rf
            rxm = FX0[t, pl.ds(at + 12, 8), :] * rf
            AYP0[t, out, :] = 1.0 + ryp
            AYM0[t, out, :] = 1.0 + rym
            RF0[t, out, :] = 2.0 * rf
            HF0[t, out, :] = 0.5 * f
            ry = 4.0 + ryp + rym
            for kind in range(3):
                if (t, kind) in ((0, 0), (3, 2)):
                    continue
                rp = rxp if kind == 2 else jnp.ones_like(rxp)
                rm = rxm if kind == 0 else jnp.ones_like(rxm)
                AXP0[3 * t + kind, out, :] = 1.0 + rp
                AXM0[3 * t + kind, out, :] = 1.0 + rm
                a = ry + rp + rm
                A0[3 * t + kind, out, :] = a
                for h in range(2):
                    INV0[h, 3 * t + kind, out, :] = jnp.where(inside, OMEGA / (a + BS0[h]), 0.0)
        return carry

    lax.fori_loop(0, 5, weights0, 0)

    for t in range(6):
        for j in range(6):
            FX1[t, 8 * j : 8 * j + 8, :] = jnp.where(
                sub < 4,
                jnp.broadcast_to(FA[2 * g + t, 4 + 2 * j : 5 + 2 * j, :], (8, 128)),
                jnp.broadcast_to(FA[2 * g + t, 5 + 2 * j : 6 + 2 * j, :], (8, 128)),
            )

    def weights1(c, carry):
        at = pl.multiple_of(8 * c, 8)
        out = pl.ds(at, 8)
        for t in range(6):
            f = FX1[t, pl.ds(at + 8, 8), :]
            inside = f > 0.0
            rf = 1.0 / jnp.where(inside, f, 1.0)
            ryp = FX1[t, pl.ds(at + 9, 8), :] * rf
            rym = FX1[t, pl.ds(at + 7, 8), :] * rf
            AYP1[t, out, :] = 1.0 + ryp
            AYM1[t, out, :] = 1.0 + rym
            RF1[t, out, :] = 8.0 * rf
            HF1[t, out, :] = 0.125 * f
            ry = 4.0 + ryp + rym
            for r in range(4):
                q = 4 * t + r - 3
                if q < 0 or q > 17:
                    continue
                rp = FX1[t + 1, pl.ds(at + 8, 8), :] * rf if r == 3 else jnp.ones_like(rf)
                rm = FX1[t - 1, pl.ds(at + 8, 8), :] * rf if r == 0 else jnp.ones_like(rf)
                AXP1[q, out, :] = 1.0 + rp
                AXM1[q, out, :] = 1.0 + rm
                a = ry + rp + rm
                A1[q, out, :] = a
                INV1[q, out, :] = jnp.where(inside, OMEGA / (a + BS[1]), 0.0)
        return carry

    lax.fori_loop(0, 4, weights1, 0)

    for copy in own:
        copy.wait()
    for copy in first0:
        copy.wait_recv()

    def kind0(q):
        t = (q + 4) // 8
        r = (q + 4) % 8
        return t, 3 * t + (r + 6) // 7 + r // 7

    def start0(q, carry):
        t, kind = kind0(q)
        for c in range(5):
            rows = pl.ds(8 * c, 8)
            rf = RF0[t, rows, :]
            for h in range(2):
                f = F0[h, q, pl.ds(8 * c + 4, 8), :]
                B0[h, q, pl.ds(8 * c + 8, 8), :] = f * INV0[h, kind, rows, :] * (rf * RP0[h])
        return carry

    def spread0(v_ref, q, t, kind, row, w_row):
        axp, axm = AXP0[kind, pl.ds(w_row, 8), :], AXM0[kind, pl.ds(w_row, 8), :]
        ayp, aym = AYP0[t, pl.ds(w_row, 8), :], AYM0[t, pl.ds(w_row, 8), :]
        centre = [v_ref[h, q, pl.ds(row, 8), :] for h in range(2)]
        up, dn = zup0(*centre), zdn0(*centre)
        total = []
        for h in range(2):
            total.append(
                axp * v_ref[h, q + 1, pl.ds(row, 8), :]
                + axm * v_ref[h, q - 1, pl.ds(row, 8), :]
                + ayp * v_ref[h, q, pl.ds(row + 1, 8), :]
                + aym * v_ref[h, q, pl.ds(row - 1, 8), :]
                + BU0[h] * up[h]
                + BD0[h] * dn[h]
            )
        return centre, total

    def relax0(src, dst, fresh):
        def body(q, carry):
            t, kind = kind0(q)
            for c in range(5):
                row = 8 * c + 8
                centre, total = spread0(src, q, t, kind, row, 8 * c)
                for h in range(2):
                    if fresh:
                        kept = (1.0 + KEEP) * centre[h]
                    else:
                        kept = KEEP * centre[h] + B0[h, q, pl.ds(row, 8), :]
                    dst[h, q, pl.ds(row, 8), :] = kept + INV0[h, kind, pl.ds(8 * c, 8), :] * total[h]
            return carry

        return body

    def left0(v_ref, q, c):
        t, kind = kind0(q)
        w_row = 8 * c + 4
        centre, total = spread0(v_ref, q, t, kind, 8 * c + 12, w_row)
        a = A0[kind, pl.ds(w_row, 8), :]
        hf = HF0[t, pl.ds(w_row, 8), :]
        left = []
        for h in range(2):
            f = F0[h, q, pl.ds(8 * c + 8, 8), :]
            left.append(f - hf * permit0[h] * ((a + BS0[h]) * centre[h] - total[h]))
        return centre, left

    lax.fori_loop(2, 22, start0, 0)
    lax.fori_loop(3, 21, relax0(B0, V0, True), 0)

    def down0(i, carry):
        for c in range(4):
            first = left0(V0, 2 * i + 4, c)[1]
            second = left0(V0, 2 * i + 5, c)[1]
            T0[i, pl.ds(8 * c, 8), :] = halves(first[0] + second[0], first[1] + second[1])
        F1[i + 5, 8:24, :] = 0.125 * (
            T0[i, pl.ds(0, 16, stride=2), :] + T0[i, pl.ds(1, 16, stride=2), :]
        )
        return carry

    lax.fori_loop(0, 8, down0, 0)
    for copy in first1 + late0:
        copy.start()

    for x in range(10):
        for j in range(5):
            rows = [jnp.broadcast_to(FA[x + 1, 4 * j + k : 4 * j + k + 1, :], (8, 128)) for k in range(4)]
            FX2[x, 8 * j : 8 * j + 8, :] = jnp.where(
                sub < 4, jnp.where(sub < 2, rows[0], rows[1]), jnp.where(sub < 6, rows[2], rows[3])
            )

    def weights2(x, carry):
        for c in range(3):
            out = pl.ds(8 * c, 8)
            f = FX2[x + 1, 8 * c + 8 : 8 * c + 16, :]
            inside = f > 0.0
            rf = 1.0 / jnp.where(inside, f, 1.0)
            ryp = FX2[x + 1, pl.ds(8 * c + 9, 8), :] * rf
            rym = FX2[x + 1, pl.ds(8 * c + 7, 8), :] * rf
            AYP2[x, out, :] = 1.0 + ryp
            AYM2[x, out, :] = 1.0 + rym
            RF2[x, out, :] = 32.0 * rf
            HF2[x, out, :] = 0.03125 * f
            ry = 4.0 + ryp + rym
            for r in range(2):
                rp = FX2[x + 2, 8 * c + 8 : 8 * c + 16, :] * rf if r == 1 else jnp.ones_like(rf)
                rm = FX2[x, 8 * c + 8 : 8 * c + 16, :] * rf if r == 0 else jnp.ones_like(rf)
                AXP2[2 * x + r, out, :] = 1.0 + rp
                AXM2[2 * x + r, out, :] = 1.0 + rm
                a = ry + rp + rm
                A2[2 * x + r, out, :] = a
                INV2[2 * x + r, out, :] = jnp.where(inside, OMEGA / (a + BS[2]), 0.0)
        return carry

    lax.fori_loop(0, 8, weights2, 0)
    for ref in (B2, V2, W2):
        for x in (0, 1, 18, 19):
            for c in range(3):
                ref[x, 8 * c : 8 * c + 8, :] = zero

    for copy in first1:
        copy.wait_recv()

    def start1(q, carry):
        t = (q + 3) // 4
        for c in range(4):
            rows = pl.ds(8 * c, 8)
            B1[q, rows, :] = F1[q, rows, :] * INV1[q, rows, :] * (RF1[t, rows, :] * RPS[1])
        return carry

    def spread1(v_ref, q, row):
        t = (q + 3) // 4
        rows = pl.ds(row, 8)
        centre = v_ref[q, rows, :]
        total = (
            AXP1[q, rows, :] * v_ref[q + 1, rows, :]
            + AXM1[q, rows, :] * v_ref[q - 1, rows, :]
            + AYP1[t, rows, :] * v_ref[q, pl.ds(row + 1, 8), :]
            + AYM1[t, rows, :] * v_ref[q, pl.ds(row - 1, 8), :]
            + BU[1] * zup(centre, 1)
            + BD[1] * zdn(centre, 1)
        )
        return centre, total

    def relax1(src, dst, fresh):
        def body(q, carry):
            for c in range(3):
                rows = pl.ds(8 * c + 4, 8)
                centre, total = spread1(src, q, 8 * c + 4)
                kept = (1.0 + KEEP) * centre if fresh else KEEP * centre + B1[q, rows, :]
                dst[q, rows, :] = kept + INV1[q, rows, :] * total
            return carry

        return body

    lax.fori_loop(3, 15, start1, 0)
    lax.fori_loop(4, 14, relax1(B1, V1, True), 0)

    def down1(i, carry):
        for c in range(2):
            rows = pl.ds(8 * c + 8, 8)
            left = []
            for q in (2 * i + 5, 2 * i + 6):
                centre, total = spread1(V1, q, 8 * c + 8)
                hp = HF1[(q + 3) // 4, rows, :] * permits[1]
                left.append(F1[q, rows, :] - hp * ((A1[q, rows, :] + BS[1]) * centre - total))
            T1[i, pl.ds(8 * c, 8), :] = pair(left[0] + left[1], 2)
        F2[4 * g + i, 8:16, :] = 0.125 * (
            T1[i, pl.ds(0, 8, stride=2), :] + T1[i, pl.ds(1, 8, stride=2), :]
        )
        return carry

    lax.fori_loop(0, 4, down1, 0)
    for copy in first2 + late1:
        copy.start()

    tiles = devs + 2

    def yup(v, after, level):
        if level == 5:
            return after
        step = 1 << (level - 2)
        return jnp.where((lane & 6) >= 8 - step, roll(after, 8 - step), roll(v, -step))

    def ydn(v, before, level):
        if level == 5:
            return before
        step = 1 << (level - 2)
        return jnp.where((lane & 6) < step, roll(before, step - 8), roll(v, step))

    for k in range(3):
        for ref in (FC, VC, WC, BC):
            ref[k, 0, :, :] = zero
            ref[k, tiles - 1, :, :] = zero
    for e in range(devs):
        cols = [jnp.broadcast_to(fills[:, 4 * e + k : 4 * e + k + 1], (8, 128)) for k in range(4)]
        low, high = (lane & 2) == 0, (lane & 4) == 0
        f = jnp.where(high, jnp.where(low, cols[0], cols[1]), jnp.where(low, cols[2], cols[3]))
        FC[0, e + 1, :, :] = f
        f = 0.25 * pair(spair(f, 1), 2)
        FC[1, e + 1, :, :] = f
        FC[2, e + 1, :, :] = 0.25 * pair(spair(f, 2), 4)

    def weights_coarse(e, carry):
        for k in range(3):
            level = k + 3
            step = 1 << k
            f = FC[k, e, :, :]
            rf = 1.0 / f
            ryp = yup(f, FC[k, e + 1, :, :], level) * rf
            rym = ydn(f, FC[k, e - 1, :, :], level) * rf
            last, first = sub >= 8 - step, sub < step
            rxp = jnp.where(last, 0.0, sroll(f, -step) * rf)
            rxm = jnp.where(first, 0.0, sroll(f, step) * rf)
            AXPC[k, e, :, :] = jnp.where(last, 0.0, 1.0 + rxp)
            AXMC[k, e, :, :] = jnp.where(first, 0.0, 1.0 + rxm)
            AYPC[k, e, :, :] = 1.0 + ryp
            AYMC[k, e, :, :] = 1.0 + rym
            a = 4.0 + ryp + rym + rxp + rxm
            AC[k, e, :, :] = a
            INVC[k, e, :, :] = OMEGA / (a + BS[level])
        return carry

    lax.fori_loop(1, devs + 1, weights_coarse, 0)

    for copy in first2:
        copy.wait_recv()

    def start2(q, carry):
        for c in range(3):
            rows = pl.ds(8 * c, 8)
            B2[q + 2, rows, :] = F2[q, rows, :] * INV2[q, rows, :] * (RF2[q // 2, rows, :] * RPS[2])
        return carry

    def spread2(v_ref, q, row):
        rows = pl.ds(row, 8)
        centre = v_ref[q + 2, rows, :]
        total = (
            AXP2[q, rows, :] * v_ref[q + 3, rows, :]
            + AXM2[q, rows, :] * v_ref[q + 1, rows, :]
            + AYP2[q // 2, rows, :] * v_ref[q + 2, pl.ds(row + 1, 8), :]
            + AYM2[q // 2, rows, :] * v_ref[q + 2, pl.ds(row - 1, 8), :]
            + BU[2] * zup(centre, 2)
            + BD[2] * zdn(centre, 2)
        )
        return centre, total

    def relax2(src, dst, fresh):
        def body(q, carry):
            for c in range(2):
                rows = pl.ds(8 * c + 4, 8)
                centre, total = spread2(src, q, 8 * c + 4)
                kept = (1.0 + KEEP) * centre if fresh else KEEP * centre + B2[q + 2, rows, :]
                dst[q + 2, rows, :] = kept + INV2[q, rows, :] * total
            return carry

        return body

    lax.fori_loop(0, 16, start2, 0)
    lax.fori_loop(0, 16, relax2(B2, V2, True), 0)
    packed = zero
    for x in range(8):
        left = []
        for q in (2 * x, 2 * x + 1):
            centre, total = spread2(V2, q, 8)
            hp = HF2[x, 8:16, :] * permits[2]
            left.append(F2[q, 8:16, :] - hp * ((A2[q, 8:16, :] + BS[2]) * centre - total))
        both = pair(left[0] + left[1], 4)
        both = jnp.where((sub & 6) == (lane & 6), both, 0.0)
        packed = jnp.where(sub == x, jnp.sum(both, axis=0, keepdims=True), packed)
    G[pl.ds(d, 1), :, :] = (0.125 * packed)[None]

    def tell(k, carry):
        pltpu.make_async_remote_copy(
            src_ref=G.at[d],
            dst_ref=G.at[d],
            send_sem=s3_send,
            recv_sem=s3_recv,
            device_id=(g, lax.rem(d + k, devs)),
            device_id_type=MESH,
        ).start()
        return carry

    lax.fori_loop(1, devs, tell, 0)

    for copy in late0:
        copy.wait_recv()
    for q in (0, 1, 22, 23):
        start0(q, 0)
    for q in (1, 2, 21, 22):
        relax0(B0, V0, True)(q, 0)
    for copy in late1:
        copy.wait_recv()
    for q in (0, 1, 2, 15, 16, 17):
        start1(q, 0)
    for q in (1, 2, 3, 14, 15, 16):
        relax1(B1, V1, True)(q, 0)

    everyone = pltpu.make_async_copy(G.at[0 : devs - 1], G.at[0 : devs - 1], s3_recv)
    everyone.wait()

    def spread_coarse(k, v_ref, e):
        level = k + 3
        step = 1 << k
        centre = v_ref[k, e, :, :]
        total = (
            AXPC[k, e, :, :] * sroll(centre, -step)
            + AXMC[k, e, :, :] * sroll(centre, step)
            + AYPC[k, e, :, :] * yup(centre, v_ref[k, e + 1, :, :], level)
            + AYMC[k, e, :, :] * ydn(centre, v_ref[k, e - 1, :, :], level)
            + BU[level] * zup(centre, level)
            + BD[level] * zdn(centre, level)
        )
        return centre, total

    per = 8 if devs % 8 == 0 else 4

    def over_tiles(body):
        def several(i, carry):
            for j in range(per):
                body(i * per + j + 1)
            return carry

        lax.fori_loop(0, devs // per, several, 0)

    def start_coarse(k, f_ref):
        factor = 2.0 * 4.0 ** (k + 3)

        def body(e):
            f = f_ref[e - 1, :, :]
            BC[k, e, :, :] = f * INVC[k, e, :, :] * (factor * RPS[k + 3]) / FC[k, e, :, :]

        over_tiles(body)

    def relax_coarse(k, src, dst, fresh=False):
        def body(e):
            centre, total = spread_coarse(k, src, e)
            kept = (1.0 + KEEP) * centre if fresh else KEEP * centre + BC[k, e, :, :]
            dst[k, e, :, :] = kept + INVC[k, e, :, :] * total

        over_tiles(body)

    def down_coarse(k, f_ref, next_ref):
        level = k + 3
        factor = 0.5 * 0.25**level

        def body(e):
            centre, total = spread_coarse(k, VC, e)
            hp = FC[k, e, :, :] * (factor * permits[level])
            left = f_ref[e - 1, :, :] - hp * ((AC[k, e, :, :] + BS[level]) * centre - total)
            left = pair(pair(spair(left, 1 << k), 1 << (k + 1)), 1 << level)
            next_ref[e - 1, :, :] = 0.125 * left

        over_tiles(body)

    for k, f_ref, next_ref in ((0, G, F4), (1, F4, F5)):
        start_coarse(k, f_ref)
        relax_coarse(k, BC, VC, fresh=True)
        down_coarse(k, f_ref, next_ref)
    start_coarse(2, F5)
    relax_coarse(2, BC, VC, fresh=True)

    def two_sweeps(i, carry):
        relax_coarse(2, VC, WC)
        relax_coarse(2, WC, VC)
        return carry

    lax.fori_loop(0, (SWEEPS - 2) // 2, two_sweeps, 0)
    for k in (1, 0):

        def correct(e):
            VC[k, e, :, :] = VC[k, e, :, :] + VC[k + 1, e, :, :]

        over_tiles(correct)
        relax_coarse(k, VC, WC)
        relax_coarse(k, WC, VC)

    yl = (lane >> 1) & 3
    for b in range(3):
        tile = VC[0, d + b, :, :]
        rolled = {s: (tile if s == 0 else roll(tile, -2 * s)) for s in range(-3, 4)}
        for k in range(4):
            UU[b, k, :, :] = jnp.where(
                yl < 2,
                jnp.where(yl == 0, rolled[k], rolled[k - 1]),
                jnp.where(yl == 2, rolled[k - 2], rolled[k - 3]),
            )
    for x in range(8):
        for b in range(3):
            rows = [jnp.broadcast_to(UU[b, k, x : x + 1, :], (8, 128)) for k in range(4)]
            fine = jnp.where(
                sub < 4, jnp.where(sub < 2, rows[0], rows[1]), jnp.where(sub < 6, rows[2], rows[3])
            )
            for q in (2 * x + 2, 2 * x + 3):
                V2[q, 8 * b : 8 * b + 8, :] = V2[q, 8 * b : 8 * b + 8, :] + fine
    lax.fori_loop(0, 16, relax2(V2, W2, False), 0)
    lax.fori_loop(0, 16, relax2(W2, V2, False), 0)

    def raise1(i, carry):
        for row, count in ((6, 8), (14, 4)):
            fine = V2[4 * g + i, pl.ds(row, count), :]
            for odd in range(2):
                P1[i, pl.ds(2 * (row - 6) + odd, count, stride=2), :] = fine
        for q in (2 * i + 1, 2 * i + 2):
            for c in range(3):
                rows = pl.ds(8 * c + 4, 8)
                V1[q, rows, :] = V1[q, rows, :] + P1[i, 8 * c : 8 * c + 8, :]
        return carry

    lax.fori_loop(0, 8, raise1, 0)
    lax.fori_loop(2, 16, relax1(V1, W1, False), 0)
    lax.fori_loop(3, 15, relax1(W1, V1, False), 0)

    def raise0(i, carry):
        for row, count in ((6, 8), (14, 8), (22, 4)):
            coarse = V1[i + 3, pl.ds(row, 8), :]
            fine = (jnp.where(even, coarse, roll(coarse, 1)), jnp.where(even, roll(coarse, -1), coarse))
            for h in range(2):
                for odd in range(2):
                    P0[h, i, pl.ds(2 * (row - 6) + odd, count, stride=2), :] = fine[h][0:count, :]
        for q in (2 * i, 2 * i + 1):
            for h in range(2):
                for c in range(5):
                    rows = pl.ds(8 * c + 8, 8)
                    V0[h, q, rows, :] = V0[h, q, rows, :] + P0[h, i, 8 * c : 8 * c + 8, :]
        return carry

    lax.fori_loop(0, 12, raise0, 0)
    lax.fori_loop(2, 22, relax0(V0, W0, False), 0)
    lax.fori_loop(3, 21, relax0(W0, V0, False), 0)

    def finish(x, carry):
        for c in range(4):
            centre, left = left0(V0, x + 4, c)
            for h in range(2):
                pot_ref[x, 8 * c : 8 * c + 8, h * 128 : h * 128 + 128] = centre[h]
                res_ref[x, 8 * c : 8 * c + 8, h * 128 : h * 128 + 128] = left[h]
        return carry

    lax.fori_loop(0, 16, finish, 0)

    for copy in first0 + late0 + first1 + late1 + first2:
        copy.wait_send()
    pltpu.make_async_copy(G.at[0 : devs - 1], G.at[0 : devs - 1], s3_send).wait()


def solution(mesh):
    groups, devs = mesh.shape["group"], mesh.shape["dev"]

    def rows(*shape):
        return pltpu.VMEM(shape + (128,), jnp.float32)

    def sems(count):
        return pltpu.SemaphoreType.DMA((count,))

    def on_device(source, plane_layer, layer_permittivity, tile_kind, kind_fill):
        vmem = pl.BlockSpec(memory_space=pltpu.VMEM)
        smem = pl.BlockSpec(memory_space=pltpu.SMEM)
        tiles = devs + 2
        coarse = rows(3, tiles, 8)
        out = jax.ShapeDtypeStruct(source.shape, jnp.float32)
        scratch = [
            rows(2, 24, 48), rows(2, 24, 56), rows(2, 24, 56), rows(2, 24, 56),
            rows(2, 12, 40), rows(12, 40), rows(12, 40), rows(12, 40),
            rows(4, 40), rows(4, 40), rows(4, 40), rows(4, 40), rows(6, 64),
            rows(8, 32), rows(2, 12, 40),
            rows(18, 32), rows(18, 32), rows(18, 32), rows(18, 32),
            rows(18, 32), rows(18, 32), rows(18, 32), rows(18, 32),
            rows(6, 32), rows(6, 32), rows(6, 32), rows(6, 32), rows(6, 48),
            rows(4, 16), rows(8, 24),
            rows(16, 24), rows(20, 24), rows(20, 24), rows(20, 24),
            rows(16, 24), rows(16, 24), rows(16, 24), rows(16, 24),
            rows(8, 24), rows(8, 24), rows(8, 24), rows(8, 24), rows(10, 40),
            rows(3, 4, 8),
            rows(12, 24), rows(devs, 8), rows(devs, 8), rows(devs, 8),
            coarse, coarse, coarse, coarse, coarse, coarse, coarse, coarse, coarse, coarse,
            sems(2), sems(18), sems(18), sems(18), sems(18), sems(9), sems(9), sems(9), sems(9),
            sems(3 * groups - 1), sems(3 * groups - 1),
            pltpu.SemaphoreType.DMA, pltpu.SemaphoreType.DMA,
        ]
        return pl.pallas_call(
            functools.partial(kernel, groups, devs),
            out_shape=(out, out),
            in_specs=[vmem, vmem, smem, smem, pl.BlockSpec(memory_space=pl.ANY)],
            out_specs=(vmem, vmem),
            scratch_shapes=scratch,
            compiler_params=pltpu.CompilerParams(
                collective_id=0, has_side_effects=True, vmem_limit_bytes=48 * 1024 * 1024
            ),
        )(plane_layer.reshape(2, 128), tile_kind, layer_permittivity, kind_fill, source)

    in_specs = (P("group", "dev", None), P(), P(), P(), P())
    out_specs = (P("group", "dev", None), P("group", "dev", None))
    return jax.shard_map(
        on_device, mesh=mesh, in_specs=in_specs, out_specs=out_specs, check_vma=False
    )
```

time: 487 us -> 71 us (0.15)
  the two profiles are of different devices: /device:TPU:22 before, /device:TPU:1 now
where the time goes in v1:
time: 71 us; the launch traced here: 70.8 us
  Pallas kernels  65.4 us (92%)
  local copies, waits for them, and re-layouts  4.65 us (7%)
    pallas_call x1, Pallas kernels, on_device(): pl.pallas_call(functools.partial(kernel, groups, devs), out_shape=(out, o...  65.4 us
    unnamed x12, local copies, waits for them, and re-layouts  4.65 us

profile of v1, /device:TPU:1, one launch (start us, length us, event | category | flops | bytes accessed | tf_op | source)
XLA Modules:
  0.0 70.8 jit_solution(2246148667354562590)
XLA Ops:
  0.6 0.0 copy-start.3
  0.6 0.0 copy-start.2
  0.7 0.6 copy-done.3
  1.3 0.0 copy-done.2
  1.3 0.0 copy-start
  1.3 1.0 %copy-done = f32[16,32,256]{2,1,0:T(8,128)S(1)} copy-done((f32[16,32,256]{2,1,0:T(8,128)S(1)}, f32[16,32,256]{2,1,0:T(8,128)}, u32[]{:S(2)}) %copy-start) | copy-done | bytes 524312
  2.4 0.0 copy-start.1
  2.4 0.7 copy-done.1
  3.1 0.0 copy-start.4
  3.1 0.7 copy-done.4
  3.7 65.4 %shard_map.68 = (f32[16,32,256]{2,1,0:T(8,128)S(1)}, f32[16,32,256]{2,1,0:T(8,128)S(1)}) custom-call(s32[2,128]{1,0:T(2,128)S(1)} %bitcast.1, s32[8,128]{1,0:T(8,128)S(1)} %copy-done.1, f32[8]{0:T(128)S(1)} %copy-done.3, f32[16]{0:T(128)S(1)} %copy-done.4, f32[16,32,256]{2,1,0:T(8,128)S(1)} %copy-done), custom_call_target="tpu_custom_call" | custom-call | tf_op jit(solution)/shard_map/pallas_call | solution.py:751
  69.2 0.8 %copy.9 = f32[16,32,256]{2,1,0:T(8,128)} copy(f32[16,32,256]{2,1,0:T(8,128)S(1)} %get-tuple-element.4) | data formatting | bytes 1048576
  70.0 0.8 %copy.10 = f32[16,32,256]{2,1,0:T(8,128)} copy(f32[16,32,256]{2,1,0:T(8,128)S(1)} %get-tuple-element.5) | data formatting | bytes 1048576
Async XLA Ops:
  0.6 0.7 copy-start.3
  0.6 0.7 copy-start.2
  1.3 1.0 %copy-start = (f32[16,32,256]{2,1,0:T(8,128)S(1)}, f32[16,32,256]{2,1,0:T(8,128)}, u32[]{:S(2)}) copy-start(f32[16,32,256]{2,1,0:T(8,128)} %source.1) | copy-start | bytes 1572868
  2.4 0.7 copy-start.1
  3.1 0.7 copy-start.4

commit v2 on v1

v2 whole, which is shorter than its diff:
```python
import functools

import jax
import jax.numpy as jnp
from jax import lax
from jax.experimental import pallas as pl
from jax.experimental.pallas import tpu as pltpu
from jax.sharding import PartitionSpec as P

MESH = pl.DeviceIdType.MESH
OMEGA = 2.0 / 3.0
KEEP = 1.0 - OMEGA
SWEEPS = 24
NEIGHBOURS = tuple(
    (dx, dy) for dx in (-1, 0, 1) for dy in (-1, 0, 1) if (dx, dy) != (0, 0)
)


def kernel(
    groups,
    devs,
    layers_hbm,
    kinds_hbm,
    permit_hbm,
    fill_hbm,
    source,
    pot_ref,
    res_ref,
    layers_ref, kinds_ref, permit_ref, fill_ref,
    F0, V0, W0, B0, INV0, A0, AXP0, AXM0, AYP0, AYM0, RF0, HF0, FX0, T0, P0,
    F1, V1, W1, B1, INV1, A1, AXP1, AXM1, AYP1, AYM1, RF1, HF1, FX1, T1, P1,
    F2, V2, W2, B2, INV2, A2, AXP2, AXM2, AYP2, AYM2, RF2, HF2, FX2, UU,
    FA, G, F3, F4, F5, FC, VC, WC, BC, INVC, AC, AXPC, AXMC, AYPC, AYMC,
    input_sem, local_sem, s0_send, s0_recv, s0l_send, s0l_recv, s1_send, s1_recv, s1l_send, s1l_recv,
    s2_send, s2_recv, s3_send, s3_recv,
):
    g = lax.axis_index("group")
    d = lax.axis_index("dev")
    f32 = jnp.float32
    lane = lax.broadcasted_iota(jnp.int32, (8, 128), 1)
    sub = lax.broadcasted_iota(jnp.int32, (8, 128), 0)
    even = (lane & 1) == 0
    zero = jnp.zeros((8, 128), f32)
    blocks = devs // 4
    counts = (4 * blocks, 2 * blocks, blocks)

    def peer(dx, dy):
        return (lax.rem(g + dx + groups, groups), lax.rem(d + dy + devs, devs))

    def roll(v, shift):
        return pltpu.roll(v, shift % 128, 1)

    def sroll(v, shift):
        return pltpu.roll(v, shift % 8, 0)

    def permute(v, index):
        return jnp.take_along_axis(v, index, axis=1, mode="promise_in_bounds")

    barrier = pltpu.get_barrier_semaphore()
    column = [(dx, dy) for dx in range(groups) for dy in (-1, 0, 1) if (dx, dy) != (0, 0)]
    for dx, dy in column:
        pl.semaphore_signal(barrier, inc=1, device_id=peer(dx, dy), device_id_type=MESH)

    def greet(k, carry):
        pl.semaphore_signal(barrier, inc=1, device_id=(g, lax.rem(d + k, devs)), device_id_type=MESH)
        return carry

    inputs = [
        pltpu.make_async_copy(src, dst, input_sem.at[i])
        for i, (src, dst) in enumerate(
            (
                (layers_hbm, layers_ref),
                (kinds_hbm, kinds_ref),
                (permit_hbm, permit_ref),
                (fill_hbm, fill_ref),
            )
        )
    ]
    own = [
        pltpu.make_async_copy(
            source.at[:, :, h * 128 : h * 128 + 128], F0.at[h, 4:20, 8:40, :], local_sem.at[h]
        )
        for h in range(2)
    ]
    for copy in inputs:
        copy.start()
    lax.fori_loop(2, devs - 1, greet, 0)
    for copy in own:
        copy.start()

    def halo0(dx, dy, h, late):
        px = {0: (0, 16, 4), 1: (14, 2, 2), -1: (0, 2, 20)}[dx]
        if late:
            px = {1: (12, 2, 0), -1: (2, 2, 22)}[dx]
        py = {0: (0, 32, 8), 1: (24, 8, 0), -1: (0, 8, 40)}[dy]
        slot = ((dx + 1) * 3 + dy + 1) * 2 + h
        send, recv = (s0l_send, s0l_recv) if late else (s0_send, s0_recv)
        return pltpu.make_async_remote_copy(
            src_ref=source.at[px[0] : px[0] + px[1], py[0] : py[0] + py[1], h * 128 : h * 128 + 128],
            dst_ref=F0.at[h, px[2] : px[2] + px[1], py[2] : py[2] + py[1], :],
            send_sem=send.at[slot],
            recv_sem=recv.at[slot],
            device_id=peer(dx, dy),
            device_id_type=MESH,
        )

    first0 = [halo0(dx, dy, h, False) for dx, dy in NEIGHBOURS for h in range(2)]
    late0 = [halo0(dx, dy, h, True) for dx, dy in NEIGHBOURS if dx for h in range(2)]

    def halo1(dx, dy, late):
        px = {0: (0, 8, 5), 1: (6, 2, 3), -1: (0, 2, 13)}[dx]
        if late:
            px = {1: (3, 3, 0), -1: (2, 3, 15)}[dx]
        py = {0: (0, 16, 8), 1: (8, 8, 0), -1: (0, 8, 24)}[dy]
        slot = (dx + 1) * 3 + dy + 1
        send, recv = (s1l_send, s1l_recv) if late else (s1_send, s1_recv)
        return pltpu.make_async_remote_copy(
            src_ref=F1.at[px[0] + 5 : px[0] + px[1] + 5, py[0] + 8 : py[0] + py[1] + 8, :],
            dst_ref=F1.at[px[2] : px[2] + px[1], py[2] : py[2] + py[1], :],
            send_sem=send.at[slot],
            recv_sem=recv.at[slot],
            device_id=peer(dx, dy),
            device_id_type=MESH,
        )

    first1 = [halo1(dx, dy, False) for dx, dy in NEIGHBOURS]
    late1 = [halo1(dx, dy, True) for dx, dy in NEIGHBOURS if dx]

    def block2(slot):
        dx, dy = column[slot]
        return pltpu.make_async_remote_copy(
            src_ref=F2.at[pl.ds(4 * g, 4), 8:16, :],
            dst_ref=F2.at[pl.ds(4 * g, 4), 8 - 8 * dy : 16 - 8 * dy, :],
            send_sem=s2_send.at[slot],
            recv_sem=s2_recv.at[slot],
            device_id=peer(dx, dy),
            device_id_type=MESH,
        )

    first2 = [block2(slot) for slot in range(len(column))]

    for copy in inputs:
        copy.wait()
    kinds = kinds_ref[...]
    fills = zero
    for kind in range(fill_ref.shape[0]):
        fills = jnp.where(kinds == kind, fill_ref[kind], fills)
    fills = jnp.where(lane < 4 * devs, fills, 0.0)
    shifted = pltpu.roll(fills, lax.rem(8 + 128 - 4 * d + 128, 128), 1)
    tile_y = 4 * d - 8 + lane
    shifted = jnp.where((tile_y >= 0) & (tile_y < 4 * devs), shifted, 0.0)
    for c in range(3):
        for x in (0, 1, 10, 11):
            FA[x, 8 * c : 8 * c + 8, :] = zero
        for x in range(8):
            row = jnp.broadcast_to(shifted[x : x + 1, :], (8, 128))
            picked = jnp.sum(jnp.where(lane == sub + 8 * c, row, 0.0), axis=1, keepdims=True)
            FA[x + 2, 8 * c : 8 * c + 8, :] = jnp.broadcast_to(picked, (8, 128))

    permit0 = []
    for h in range(2):
        layer = jnp.broadcast_to(layers_ref[h : h + 1, :], (8, 128))
        value = zero
        for k in range(permit_ref.shape[0]):
            value = jnp.where(layer == k, permit_ref[k], value)
        permit0.append(value)

    def zup0(h0, h1):
        r0, r1 = roll(h0, -1), roll(h1, -1)
        return jnp.where(lane == 127, r1, r0), r1

    def zdn0(h0, h1):
        r0, r1 = roll(h0, 1), roll(h1, 1)
        return r0, jnp.where(lane == 0, r0, r1)

    def zup(v, level):
        return roll(v, -(1 << (level - 1)))

    def zdn(v, level):
        return roll(v, 1 << (level - 1))

    def pair(v, step):
        return v + jnp.where((lane & step) == 0, roll(v, -step), roll(v, step))

    def spair(v, step):
        return v + jnp.where((sub & step) == 0, sroll(v, -step), sroll(v, step))

    gather_z = jnp.where(lane < 64, 2 * lane, 2 * lane - 127)
    low_z = lane >> 1
    high_z = low_z + 64

    def halves(h0, h1):
        both = jnp.where(even, h0, h1) + jnp.where(even, roll(h0, -1), roll(h1, 1))
        return permute(both, gather_z)

    pu0, pu1 = zup0(*permit0)
    pd0, pd1 = zdn0(*permit0)
    RP0 = [1.0 / p for p in permit0]
    ru = [pu0 * RP0[0], jnp.where(lane == 127, 0.0, pu1 * RP0[1])]
    rd = [jnp.where(lane == 0, 0.0, pd0 * RP0[0]), pd1 * RP0[1]]
    BU0 = [0.5 + 0.5 * ru[0], jnp.where(lane == 127, 0.0, 0.5 + 0.5 * ru[1])]
    BD0 = [jnp.where(lane == 0, 0.0, 0.5 + 0.5 * rd[0]), 0.5 + 0.5 * rd[1]]
    BS0 = [1.0 + 0.5 * (ru[h] + rd[h]) for h in range(2)]
    permits = [None, 0.5 * halves(*permit0)]
    for level in (2, 3, 4, 5):
        permits.append(0.5 * pair(permits[level - 1], 1 << (level - 2)))
    RPS, BU, BD, BS = [None], [None], [None], [None]
    for level in range(1, 6):
        p = permits[level]
        step = 1 << (level - 1)
        rp = 1.0 / p
        top, bottom = lane >= 128 - step, lane < step
        up = jnp.where(top, 0.0, zup(p, level) * rp)
        dn = jnp.where(bottom, 0.0, zdn(p, level) * rp)
        RPS.append(rp)
        BU.append(jnp.where(top, 0.0, 0.5 + 0.5 * up))
        BD.append(jnp.where(bottom, 0.0, 0.5 + 0.5 * dn))
        BS.append(1.0 + 0.5 * (up + dn))

    for t in range(6):
        for j in range(8):
            FX0[t, 8 * j : 8 * j + 8, :] = jnp.broadcast_to(FA[2 * g + t, 6 + j : 7 + j, :], (8, 128))

    def half(ratio):
        return 0.5 + 0.5 * ratio

    for c in range(5):
        at = 8 * c
        out = pl.ds(at, 8)
        for t in range(4):
            f = FX0[t + 1, pl.ds(at + 12, 8), :]
            inside = f > 0.0
            rf = 1.0 / jnp.where(inside, f, 1.0)
            ayp = half(FX0[t + 1, pl.ds(at + 13, 8), :] * rf)
            aym = half(FX0[t + 1, pl.ds(at + 11, 8), :] * rf)
            axp = half(FX0[t + 2, pl.ds(at + 12, 8), :] * rf)
            axm = half(FX0[t, pl.ds(at + 12, 8), :] * rf)
            AYP0[t, out, :] = ayp
            AYM0[t, out, :] = aym
            AXP0[t, out, :] = axp
            AXM0[t, out, :] = axm
            RF0[t, out, :] = rf
            HF0[t, out, :] = f
            for kind in range(3):
                if (t, kind) in ((0, 0), (3, 2)):
                    continue
                a = ayp + aym + (axp if kind == 2 else 1.0) + (axm if kind == 0 else 1.0)
                A0[3 * t + kind, out, :] = a
                for h in range(2):
                    INV0[h, 3 * t + kind, out, :] = jnp.where(inside, OMEGA / (a + BS0[h]), 0.0)

    pl.semaphore_wait(barrier, len(column) + devs - 3)
    for copy in first0:
        copy.start()

    for t in range(6):
        for j in range(6):
            FX1[t, 8 * j : 8 * j + 8, :] = jnp.where(
                sub < 4,
                jnp.broadcast_to(FA[2 * g + t, 4 + 2 * j : 5 + 2 * j, :], (8, 128)),
                jnp.broadcast_to(FA[2 * g + t, 5 + 2 * j : 6 + 2 * j, :], (8, 128)),
            )

    def weights1(c, carry):
        at = pl.multiple_of(8 * c, 8)
        out = pl.ds(at, 8)
        for t in range(6):
            f = FX1[t, pl.ds(at + 8, 8), :]
            inside = f > 0.0
            rf = 1.0 / jnp.where(inside, f, 1.0)
            ayp = half(FX1[t, pl.ds(at + 9, 8), :] * rf)
            aym = half(FX1[t, pl.ds(at + 7, 8), :] * rf)
            AYP1[t, out, :] = ayp
            AYM1[t, out, :] = aym
            RF1[t, out, :] = 4.0 * rf
            HF1[t, out, :] = 0.25 * f
            ay = ayp + aym
            axp = half(FX1[t + 1, pl.ds(at + 8, 8), :] * rf) if t < 5 else None
            axm = half(FX1[t - 1, pl.ds(at + 8, 8), :] * rf) if t > 0 else None
            if t < 5:
                AXP1[t, out, :] = axp
            if t > 0:
                AXM1[t, out, :] = axm
            for r in range(4):
                q = 4 * t + r - 3
                if q < 0 or q > 17 or r == 2:
                    continue
                a = ay + (axp if r == 3 else 1.0) + (axm if r == 0 else 1.0)
                A1[3 * t + min(r, 2), out, :] = a
                INV1[3 * t + min(r, 2), out, :] = jnp.where(inside, OMEGA / (a + BS[1]), 0.0)
        return carry

    lax.fori_loop(0, 4, weights1, 0)

    for x in range(10):
        for j in range(5):
            rows = [jnp.broadcast_to(FA[x + 1, 4 * j + k : 4 * j + k + 1, :], (8, 128)) for k in range(4)]
            FX2[x, 8 * j : 8 * j + 8, :] = jnp.where(
                sub < 4, jnp.where(sub < 2, rows[0], rows[1]), jnp.where(sub < 6, rows[2], rows[3])
            )

    def weights2(x, carry):
        for c in range(3):
            out = pl.ds(8 * c, 8)
            f = FX2[x + 1, 8 * c + 8 : 8 * c + 16, :]
            inside = f > 0.0
            rf = 1.0 / jnp.where(inside, f, 1.0)
            ayp = half(FX2[x + 1, pl.ds(8 * c + 9, 8), :] * rf)
            aym = half(FX2[x + 1, pl.ds(8 * c + 7, 8), :] * rf)
            axp = half(FX2[x + 2, 8 * c + 8 : 8 * c + 16, :] * rf)
            axm = half(FX2[x, 8 * c + 8 : 8 * c + 16, :] * rf)
            AYP2[x, out, :] = ayp
            AYM2[x, out, :] = aym
            AXP2[x, out, :] = axp
            AXM2[x, out, :] = axm
            RF2[x, out, :] = 16.0 * rf
            HF2[x, out, :] = 0.0625 * f
            for r in range(2):
                a = ayp + aym + (axp if r == 1 else axm) + 1.0
                A2[2 * x + r, out, :] = a
                INV2[2 * x + r, out, :] = jnp.where(inside, OMEGA / (a + BS[2]), 0.0)
        return carry

    lax.fori_loop(0, 8, weights2, 0)
    for ref in (B2, V2, W2):
        for x in (0, 1, 18, 19):
            for c in range(3):
                ref[x, 8 * c : 8 * c + 8, :] = zero

    def kind0(q):
        t, r = (q + 4) // 8, (q + 4) % 8
        kind = 0 if r == 0 else 2 if r == 7 else 1
        return t, kind, 3 * t + kind

    def start0(q, y, count):
        t, _, cls = kind0(q)
        w = pl.ds(y + 4, count)
        rf = RF0[t, w, :]
        for h in range(2):
            f = F0[h, q, pl.ds(y + 8, count), :]
            B0[h, q, pl.ds(y + 12, count), :] = f * INV0[h, cls, w, :] * (rf * RP0[h][0:count, :])

    def weighted(weight, v):
        return v if weight is None else weight * v

    def spread0(v_ref, q, y):
        t, kind, _ = kind0(q)
        w = pl.ds(y + 4, 8)
        axp = AXP0[t, w, :] if kind == 2 else None
        axm = AXM0[t, w, :] if kind == 0 else None
        ayp, aym = AYP0[t, w, :], AYM0[t, w, :]
        centre = [v_ref[h, q, pl.ds(y + 12, 8), :] for h in range(2)]
        up, dn = zup0(*centre), zdn0(*centre)
        total = []
        for h in range(2):
            total.append(
                weighted(axp, v_ref[h, q + 1, pl.ds(y + 12, 8), :])
                + weighted(axm, v_ref[h, q - 1, pl.ds(y + 12, 8), :])
                + ayp * v_ref[h, q, pl.ds(y + 13, 8), :]
                + aym * v_ref[h, q, pl.ds(y + 11, 8), :]
                + BU0[h] * up[h]
                + BD0[h] * dn[h]
            )
        return centre, total

    def relax0(src, dst, fresh, q, c):
        cls = kind0(q)[2]
        y = 8 * c - 4
        centre, total = spread0(src, q, y)
        for h in range(2):
            if fresh:
                kept = (1.0 + KEEP) * centre[h]
            else:
                kept = KEEP * centre[h] + B0[h, q, pl.ds(y + 12, 8), :]
            dst[h, q, pl.ds(y + 12, 8), :] = kept + INV0[h, cls, pl.ds(y + 4, 8), :] * total[h]

    def left0(v_ref, q, c):
        t, _, cls = kind0(q)
        centre, total = spread0(v_ref, q, 8 * c)
        a = A0[cls, pl.ds(8 * c + 4, 8), :]
        hf = HF0[t, pl.ds(8 * c + 4, 8), :]
        left = []
        for h in range(2):
            f = F0[h, q, pl.ds(8 * c + 8, 8), :]
            left.append(f - hf * permit0[h] * ((a + BS0[h]) * centre[h] - total[h]))
        return centre, left

    for copy in own:
        copy.wait()
    for q in range(4, 20):
        for c in range(4):
            start0(q, 8 * c, 8)
    for q in range(5, 19):
        for c in range(1, 4):
            relax0(B0, V0, True, q, c)
    for copy in first0:
        copy.wait_recv()
    for q in range(2, 22):
        if 4 <= q < 20:
            start0(q, -4, 4)
            start0(q, 32, 4)
        else:
            for c in range(5):
                start0(q, 8 * c - 4, 8)
    for q in range(3, 21):
        for c in (0, 4) if 5 <= q < 19 else range(5):
            relax0(B0, V0, True, q, c)

    for i in range(8):
        for c in range(4):
            first = left0(V0, 2 * i + 4, c)[1]
            second = left0(V0, 2 * i + 5, c)[1]
            for h in range(2):
                T0[i, h, pl.ds(8 * c, 8), :] = first[h] + second[h]
        for c in range(2):
            both = [
                T0[i, h, pl.ds(16 * c, 8, stride=2), :] + T0[i, h, pl.ds(16 * c + 1, 8, stride=2), :]
                for h in range(2)
            ]
            F1[i + 5, 8 * c + 8 : 8 * c + 16, :] = 0.125 * halves(*both)
    for copy in first1 + late0:
        copy.start()

    for copy in first1:
        copy.wait_recv()

    def kind1(q):
        t, r = (q + 3) // 4, (q + 3) % 4
        return t, r, 3 * t + (0, 1, 1, 2)[r]

    def start1(q):
        t, _, cls = kind1(q)
        for c in range(4):
            rows = pl.ds(8 * c, 8)
            B1[q, rows, :] = F1[q, rows, :] * INV1[cls, rows, :] * (RF1[t, rows, :] * RPS[1])

    def spread1(v_ref, q, row):
        t, r, _ = kind1(q)
        rows = pl.ds(row, 8)
        axp = AXP1[t, rows, :] if r == 3 else None
        axm = AXM1[t, rows, :] if r == 0 else None
        centre = v_ref[q, rows, :]
        total = (
            weighted(axp, v_ref[q + 1, rows, :])
            + weighted(axm, v_ref[q - 1, rows, :])
            + AYP1[t, rows, :] * v_ref[q, pl.ds(row + 1, 8), :]
            + AYM1[t, rows, :] * v_ref[q, pl.ds(row - 1, 8), :]
            + BU[1] * zup(centre, 1)
            + BD[1] * zdn(centre, 1)
        )
        return centre, total

    def relax1(src, dst, fresh, q):
        cls = kind1(q)[2]
        for c in range(3):
            rows = pl.ds(8 * c + 4, 8)
            centre, total = spread1(src, q, 8 * c + 4)
            kept = (1.0 + KEEP) * centre if fresh else KEEP * centre + B1[q, rows, :]
            dst[q, rows, :] = kept + INV1[cls, rows, :] * total

    for q in range(3, 15):
        start1(q)
    for q in range(4, 14):
        relax1(B1, V1, True, q)
    for i in range(4):
        for c in range(2):
            rows = pl.ds(8 * c + 8, 8)
            left = []
            for q in (2 * i + 5, 2 * i + 6):
                t, _, cls = kind1(q)
                centre, total = spread1(V1, q, 8 * c + 8)
                hp = HF1[t, rows, :] * permits[1]
                left.append(F1[q, rows, :] - hp * ((A1[cls, rows, :] + BS[1]) * centre - total))
            T1[i, pl.ds(8 * c, 8), :] = left[0] + left[1]
        both = T1[i, pl.ds(0, 8, stride=2), :] + T1[i, pl.ds(1, 8, stride=2), :]
        F2[4 * g + i, 8:16, :] = 0.125 * pair(both, 1)
    for copy in first2 + late1:
        copy.start()

    for copy in first2:
        copy.wait_recv()

    def start2(q):
        for c in range(3):
            rows = pl.ds(8 * c, 8)
            B2[q + 2, rows, :] = F2[q, rows, :] * INV2[q, rows, :] * (RF2[q // 2, rows, :] * RPS[2])

    def spread2(v_ref, q, row):
        rows = pl.ds(row, 8)
        x = q // 2
        centre = v_ref[q + 2, rows, :]
        total = (
            weighted(AXP2[x, rows, :] if q % 2 else None, v_ref[q + 3, rows, :])
            + weighted(None if q % 2 else AXM2[x, rows, :], v_ref[q + 1, rows, :])
            + AYP2[x, rows, :] * v_ref[q + 2, pl.ds(row + 1, 8), :]
            + AYM2[x, rows, :] * v_ref[q + 2, pl.ds(row - 1, 8), :]
            + BU[2] * zup(centre, 2)
            + BD[2] * zdn(centre, 2)
        )
        return centre, total

    def relax2(src, dst, fresh):
        for q in range(16):
            for c in range(2):
                rows = pl.ds(8 * c + 4, 8)
                centre, total = spread2(src, q, 8 * c + 4)
                kept = (1.0 + KEEP) * centre if fresh else KEEP * centre + B2[q + 2, rows, :]
                dst[q + 2, rows, :] = kept + INV2[q, rows, :] * total

    for q in range(16):
        start2(q)
    relax2(B2, V2, True)
    place = (sub >> 1) + lax.div(d, blocks)
    packed = zero
    for x in range(8):
        left = []
        for q in (2 * x, 2 * x + 1):
            centre, total = spread2(V2, q, 8)
            hp = HF2[x, 8:16, :] * permits[2]
            left.append(F2[q, 8:16, :] - hp * ((A2[q, 8:16, :] + BS[2]) * centre - total))
        both = pair(left[0] + left[1], 2)
        both = jnp.where(((place ^ lane) & 3) == 0, both, 0.0)
        packed = jnp.where(sub == x, jnp.sum(both, axis=0, keepdims=True), packed)
    G[pl.ds(d, 1), :, :] = (0.125 * packed)[None]

    def tell(k, carry):
        pltpu.make_async_remote_copy(
            src_ref=G.at[d],
            dst_ref=G.at[d],
            send_sem=s3_send,
            recv_sem=s3_recv,
            device_id=(g, lax.rem(d + k, devs)),
            device_id_type=MESH,
        ).start()
        return carry

    lax.fori_loop(1, devs, tell, 0)

    def wrap(k, ref):
        count = counts[k]
        ref[k, 0, :, :] = jnp.where((lane & 3) == 0, 0.0, roll(ref[k, count, :, :], 1))
        ref[k, count + 1, :, :] = jnp.where((lane & 3) == 3, 0.0, roll(ref[k, 1, :, :], -1))

    for e in range(counts[0]):
        FC[0, e + 1, :, :] = permute(fills, counts[0] * (lane & 3) + e)
    for e in range(counts[1]):
        FC[1, e + 1, :, :] = 0.25 * spair(FC[0, 2 * e + 1, :, :] + FC[0, 2 * e + 2, :, :], 1)
    for e in range(counts[2]):
        FC[2, e + 1, :, :] = 0.25 * spair(FC[1, 2 * e + 1, :, :] + FC[1, 2 * e + 2, :, :], 2)
    for k in range(3):
        wrap(k, FC)
        level = k + 3
        step = 1 << k
        last, first = sub >= 8 - step, sub < step
        for e in range(1, counts[k] + 1):
            f = FC[k, e, :, :]
            rf = 1.0 / f
            ayp = half(FC[k, e + 1, :, :] * rf)
            aym = half(FC[k, e - 1, :, :] * rf)
            axp = half(jnp.where(last, 0.0, sroll(f, -step) * rf))
            axm = half(jnp.where(first, 0.0, sroll(f, step) * rf))
            AYPC[k, e, :, :] = ayp
            AYMC[k, e, :, :] = aym
            if k == 2:
                AXPC[k, e, :, :] = jnp.where(last, axm, axp)
            else:
                AXPC[k, e, :, :] = jnp.where(last, 0.0, axp)
                AXMC[k, e, :, :] = jnp.where(first, 0.0, axm)
            a = ayp + aym + axp + axm
            AC[k, e, :, :] = a
            inv = OMEGA / (a + BS[level])
            INVC[k, e, :, :] = inv
            WC[k, e, :, :] = inv * rf * (4.0**level * RPS[level])

    for copy in late0:
        copy.wait_recv()
    for q in (0, 1, 22, 23):
        for c in range(5):
            start0(q, 8 * c - 4, 8)
    for q in (1, 2, 21, 22):
        for c in range(5):
            relax0(B0, V0, True, q, c)
    for copy in late1:
        copy.wait_recv()
    for q in (0, 1, 2, 15, 16, 17):
        start1(q)
    for q in (1, 2, 3, 14, 15, 16):
        relax1(B1, V1, True, q)

    pltpu.make_async_copy(G.at[0 : devs - 1], G.at[0 : devs - 1], s3_recv).wait()

    spot = lane & 3
    for m in range(blocks):
        parts = [G[b * blocks + m, :, :] for b in range(4)]
        for y in range(4):
            pick = [parts[(p - y) % 4] for p in range(4)]
            v = jnp.where(spot < 2, jnp.where(spot == 0, pick[0], pick[1]), jnp.where(spot == 2, pick[2], pick[3]))
            if y:
                v = jnp.where(spot + y < 4, roll(v, -y), roll(v, 4 - y))
            F3[4 * m + y, :, :] = v

    def spread_coarse(k, v_ref, e):
        level = k + 3
        step = 1 << k
        centre = v_ref[k, e, :, :]
        total = (
            AXPC[k, e, :, :] * sroll(centre, -step)
            + AXMC[k, e, :, :] * sroll(centre, step)
            + AYPC[k, e, :, :] * v_ref[k, e + 1, :, :]
            + AYMC[k, e, :, :] * v_ref[k, e - 1, :, :]
            + BU[level] * zup(centre, level)
            + BD[level] * zdn(centre, level)
        )
        return centre, total

    def start_coarse(k, f_ref):
        for e in range(1, counts[k] + 1):
            BC[k, e, :, :] = f_ref[e - 1, :, :] * WC[k, e, :, :]
        wrap(k, BC)

    def relax_coarse(k, src, dst, fresh=False):
        for e in range(1, counts[k] + 1):
            centre, total = spread_coarse(k, src, e)
            kept = (1.0 + KEEP) * centre if fresh else KEEP * centre + BC[k, e, :, :]
            dst[k, e, :, :] = kept + INVC[k, e, :, :] * total
        wrap(k, dst)

    def down_coarse(k, f_ref, next_ref):
        level = k + 3
        for e in range(counts[k + 1]):
            left = []
            for q in (2 * e + 1, 2 * e + 2):
                centre, total = spread_coarse(k, VC, q)
                hp = FC[k, q, :, :] * (0.25**level * permits[level])
                left.append(f_ref[q - 1, :, :] - hp * ((AC[k, q, :, :] + BS[level]) * centre - total))
            next_ref[e, :, :] = 0.125 * pair(spair(left[0] + left[1], 1 << k), 1 << (level - 1))

    for k, f_ref, next_ref in ((0, F3, F4), (1, F4, F5)):
        start_coarse(k, f_ref)
        relax_coarse(k, BC, VC, fresh=True)
        down_coarse(k, f_ref, next_ref)
    start_coarse(2, F5)

    def sweep(i, values):
        before = jnp.where(spot == 0, 0.0, roll(values[-1], 1))
        after = jnp.where(spot == 3, 0.0, roll(values[0], -1))
        padded = (before,) + tuple(values) + (after,)
        out = []
        for e in range(1, counts[2] + 1):
            centre = padded[e]
            total = (
                AXPC[2, e, :, :] * sroll(centre, 4)
                + AYPC[2, e, :, :] * padded[e + 1]
                + AYMC[2, e, :, :] * padded[e - 1]
                + BU[5] * zup(centre, 5)
                + BD[5] * zdn(centre, 5)
            )
            out.append(KEEP * centre + BC[2, e, :, :] + INVC[2, e, :, :] * total)
        return tuple(out)

    values = tuple(BC[2, e, :, :] for e in range(1, counts[2] + 1))
    values = lax.fori_loop(0, SWEEPS - 1, sweep, values)
    for e in range(1, counts[2] + 1):
        VC[2, e, :, :] = values[e - 1]
    for k in (1, 0):
        for e in range(counts[k]):
            VC[k, e + 1, :, :] = VC[k, e + 1, :, :] + VC[k + 1, e // 2 + 1, :, :]
        wrap(k, VC)
        relax_coarse(k, VC, WC)
        relax_coarse(k, WC, VC)

    for j in range(8):
        y = 4 * d + j - 2
        inside = (y >= 0) & (y < 4 * devs)
        y = jnp.minimum(jnp.maximum(y, 0), 4 * devs - 1)
        tile = VC[0, lax.rem(y, counts[0]) + 1, :, :]
        mine = jnp.where(inside, lax.div(y, counts[0]), 4)
        UU[j, :, :] = pair(pair(jnp.where(spot == mine, tile, 0.0), 1), 2)
    for x in range(8):
        for c in range(2):
            rows = [jnp.broadcast_to(UU[4 * c + k, x : x + 1, :], (8, 128)) for k in range(4)]
            fine = jnp.where(
                sub < 4, jnp.where(sub < 2, rows[0], rows[1]), jnp.where(sub < 6, rows[2], rows[3])
            )
            at = pl.ds(8 * c + 4, 8)
            for q in (2 * x + 2, 2 * x + 3):
                V2[q, at, :] = V2[q, at, :] + fine
    relax2(V2, W2, False)
    relax2(W2, V2, False)

    for i in range(8):
        for row, count in ((6, 8), (14, 4)):
            fine = V2[4 * g + i, pl.ds(row, count), :]
            for odd in range(2):
                P1[i, pl.ds(2 * (row - 6) + odd, count, stride=2), :] = fine
        for q in (2 * i + 1, 2 * i + 2):
            for c in range(3):
                rows = pl.ds(8 * c + 4, 8)
                V1[q, rows, :] = V1[q, rows, :] + P1[i, 8 * c : 8 * c + 8, :]
    for q in range(2, 16):
        relax1(V1, W1, False, q)
    for q in range(3, 15):
        relax1(W1, V1, False, q)

    for i in range(12):
        for row, count in ((6, 8), (14, 8), (22, 4)):
            coarse = V1[i + 3, pl.ds(row, 8), :]
            fine = (permute(coarse, low_z), permute(coarse, high_z))
            for h in range(2):
                for odd in range(2):
                    P0[h, i, pl.ds(2 * (row - 6) + odd, count, stride=2), :] = fine[h][0:count, :]
        for q in (2 * i, 2 * i + 1):
            if not 1 <= q <= 22:
                continue
            for h in range(2):
                for c in range(5):
                    rows = pl.ds(8 * c + 8, 8)
                    V0[h, q, rows, :] = V0[h, q, rows, :] + P0[h, i, 8 * c : 8 * c + 8, :]
    for q in range(2, 22):
        for c in range(5):
            relax0(V0, W0, False, q, c)
    for q in range(3, 21):
        for c in range(5):
            relax0(W0, V0, False, q, c)

    for x in range(16):
        for c in range(4):
            centre, left = left0(V0, x + 4, c)
            for h in range(2):
                pot_ref[x, 8 * c : 8 * c + 8, h * 128 : h * 128 + 128] = centre[h]
                res_ref[x, 8 * c : 8 * c + 8, h * 128 : h * 128 + 128] = left[h]

    for copy in first0 + late0 + first1 + late1 + first2:
        copy.wait_send()
    pltpu.make_async_copy(G.at[0 : devs - 1], G.at[0 : devs - 1], s3_send).wait()


def solution(mesh):
    groups, devs = mesh.shape["group"], mesh.shape["dev"]

    def rows(*shape):
        return pltpu.VMEM(shape + (128,), jnp.float32)

    def sems(count):
        return pltpu.SemaphoreType.DMA((count,))

    def on_device(source, plane_layer, layer_permittivity, tile_kind, kind_fill):
        vmem = pl.BlockSpec(memory_space=pltpu.VMEM)
        hbm = pl.BlockSpec(memory_space=pl.ANY)
        tiles = devs + 2
        coarse = rows(3, tiles, 8)
        out = jax.ShapeDtypeStruct(source.shape, jnp.float32)
        scratch = [
            pltpu.VMEM((2, 128), jnp.int32), pltpu.VMEM(tile_kind.shape, jnp.int32),
            pltpu.SMEM(layer_permittivity.shape, jnp.float32), pltpu.SMEM(kind_fill.shape, jnp.float32),
            rows(2, 24, 48), rows(2, 24, 56), rows(2, 24, 56), rows(2, 24, 56),
            rows(2, 12, 40), rows(12, 40), rows(4, 40), rows(4, 40),
            rows(4, 40), rows(4, 40), rows(4, 40), rows(4, 40), rows(6, 64),
            rows(8, 2, 32), rows(2, 12, 40),
            rows(18, 32), rows(18, 32), rows(18, 32), rows(18, 32),
            rows(18, 32), rows(18, 32), rows(6, 32), rows(6, 32),
            rows(6, 32), rows(6, 32), rows(6, 32), rows(6, 32), rows(6, 48),
            rows(4, 16), rows(8, 24),
            rows(16, 24), rows(20, 24), rows(20, 24), rows(20, 24),
            rows(16, 24), rows(16, 24), rows(8, 24), rows(8, 24),
            rows(8, 24), rows(8, 24), rows(8, 24), rows(8, 24), rows(10, 40),
            rows(8, 8),
            rows(12, 24), rows(devs, 8), rows(devs, 8), rows(devs // 2, 8), rows(devs // 4, 8),
            coarse, coarse, coarse, coarse, coarse, coarse, coarse, coarse, coarse, coarse,
            sems(4), sems(2), sems(18), sems(18), sems(18), sems(18), sems(9), sems(9), sems(9), sems(9),
            sems(3 * groups - 1), sems(3 * groups - 1),
            pltpu.SemaphoreType.DMA, pltpu.SemaphoreType.DMA,
        ]
        return pl.pallas_call(
            functools.partial(kernel, groups, devs),
            out_shape=(out, out),
            in_specs=[hbm] * 5,
            out_specs=(vmem, vmem),
            scratch_shapes=scratch,
            compiler_params=pltpu.CompilerParams(
                collective_id=0, has_side_effects=True, vmem_limit_bytes=60 * 1024 * 1024
            ),
        )(plane_layer.reshape(2, 128), tile_kind, layer_permittivity, kind_fill, source)

    in_specs = (P("group", "dev", None), P(), P(), P(), P())
    out_specs = (P("group", "dev", None), P("group", "dev", None))
    return jax.shard_map(
        on_device, mesh=mesh, in_specs=in_specs, out_specs=out_specs, check_vma=False
    )
```

time: 71 us -> 42.5 us (0.60)
  Pallas kernels: 65.4 us -> 39 us
  local copies, waits for them, and re-layouts: 4.65 us -> 2.74 us
    pallas_call x1, Pallas kernels: 65.4 us -> 39 us  [on_device(): pl.pallas_call(functools.partial(kernel, groups, devs), out_shape=(out, o...]
    unnamed x12 -> x4, local copies, waits for them, and re-layouts: 4.65 us -> 2.74 us
where the time goes in v2:
time: 42.5 us; the launch traced here: 42.3 us
  Pallas kernels  39 us (92%)
  local copies, waits for them, and re-layouts  2.74 us (6%)
  between operations  0.65 us (2%)
    pallas_call x1, Pallas kernels, on_device(): pl.pallas_call(functools.partial(kernel, groups, devs), out_shape=(out, o...  39 us
    unnamed x4, local copies, waits for them, and re-layouts  2.74 us

profile of v2, /device:TPU:1, one launch (start us, length us, event | category | flops | bytes accessed | tf_op | source)
XLA Modules:
  0.0 42.3 jit_solution(4310281052499034375)
XLA Ops:
  0.6 39.0 %shard_map.68 = (f32[16,32,256]{2,1,0:T(8,128)}, f32[16,32,256]{2,1,0:T(8,128)}) custom-call(s32[2,128]{1,0:T(2,128)} %bitcast.1, s32[8,128]{1,0:T(8,128)} %kinds_hbm.1, f32[8]{0:T(128)} %permit_hbm.1, f32[16]{0:T(128)} %fill_hbm.1, f32[16,32,256]{2,1,0:T(8,128)} %source.1), custom_call_target="tpu_custom_call" | custom-call | tf_op jit(solution)/shard_map/pallas_call | solution.py:774
  39.6 0.0 copy-start
  39.6 1.9 %copy.9 = f32[16,32,256]{2,1,0:T(8,128)} copy(f32[16,32,256]{2,1,0:T(8,128)} %get-tuple-element.4) | data formatting | bytes 1048576
  41.5 0.0 copy-done
  41.6 0.8 %copy.10 = f32[16,32,256]{2,1,0:T(8,128)} copy(f32[16,32,256]{2,1,0:T(8,128)S(1)} %copy-done) | data formatting | bytes 1048576
Async XLA Ops:
  39.6 2.0 %copy-start = (f32[16,32,256]{2,1,0:T(8,128)S(1)}, f32[16,32,256]{2,1,0:T(8,128)}, u32[]{:S(2)}) copy-start(f32[16,32,256]{2,1,0:T(8,128)} %get-tuple-element.5) | copy-start | bytes 1572868

commit v3 on v2

--- a/solution.py
+++ b/solution.py
@@ -11,9 +11,7 @@
 OMEGA = 2.0 / 3.0
 KEEP = 1.0 - OMEGA
 SWEEPS = 24
-NEIGHBOURS = tuple(
-    (dx, dy) for dx in (-1, 0, 1) for dy in (-1, 0, 1) if (dx, dy) != (0, 0)
-)
+NEIGHBOURS = ((-1, -1), (1, 1), (-1, 1), (1, -1), (-1, 0), (1, 0), (0, -1), (0, 1))
 
 
 def kernel(
@@ -29,7 +27,7 @@
     layers_ref, kinds_ref, permit_ref, fill_ref,
     F0, V0, W0, B0, INV0, A0, AXP0, AXM0, AYP0, AYM0, RF0, HF0, FX0, T0, P0,
     F1, V1, W1, B1, INV1, A1, AXP1, AXM1, AYP1, AYM1, RF1, HF1, FX1, T1, P1,
-    F2, V2, W2, B2, INV2, A2, AXP2, AXM2, AYP2, AYM2, RF2, HF2, FX2, UU,
+    F2, F2P, V2, W2, B2, INV2, A2, AXP2, AXM2, AYP2, AYM2, RF2, HF2, FX2, UU,
     FA, G, F3, F4, F5, FC, VC, WC, BC, INVC, AC, AXPC, AXMC, AYPC, AYMC,
     input_sem, local_sem, s0_send, s0_recv, s0l_send, s0l_recv, s1_send, s1_recv, s1l_send, s1l_recv,
     s2_send, s2_recv, s3_send, s3_recv,
@@ -129,8 +127,8 @@
     def block2(slot):
         dx, dy = column[slot]
         return pltpu.make_async_remote_copy(
-            src_ref=F2.at[pl.ds(4 * g, 4), 8:16, :],
-            dst_ref=F2.at[pl.ds(4 * g, 4), 8 - 8 * dy : 16 - 8 * dy, :],
+            src_ref=F2P.at[pl.ds(2 * g, 2), 8:16, :],
+            dst_ref=F2P.at[pl.ds(2 * g, 2), 8 - 8 * dy : 16 - 8 * dy, :],
             send_sem=s2_send.at[slot],
             recv_sem=s2_recv.at[slot],
             device_id=peer(dx, dy),
@@ -250,7 +248,7 @@
                     INV0[h, 3 * t + kind, out, :] = jnp.where(inside, OMEGA / (a + BS0[h]), 0.0)
 
     pl.semaphore_wait(barrier, len(column) + devs - 3)
-    for copy in first0:
+    for copy in first0 + late0:
         copy.start()
 
     for t in range(6):
@@ -393,6 +391,15 @@
     for q in range(5, 19):
         for c in range(1, 4):
             relax0(B0, V0, True, q, c)
+    def down0(i, c):
+        first = left0(V0, 2 * i + 4, c)[1]
+        second = left0(V0, 2 * i + 5, c)[1]
+        for h in range(2):
+            T0[i, h, pl.ds(8 * c, 8), :] = first[h] + second[h]
+
+    for i in range(1, 7):
+        for c in (1, 2):
+            down0(i, c)
     for copy in first0:
         copy.wait_recv()
     for q in range(2, 22):
@@ -407,18 +414,15 @@
             relax0(B0, V0, True, q, c)
 
     for i in range(8):
-        for c in range(4):
-            first = left0(V0, 2 * i + 4, c)[1]
-            second = left0(V0, 2 * i + 5, c)[1]
-            for h in range(2):
-                T0[i, h, pl.ds(8 * c, 8), :] = first[h] + second[h]
+        for c in (0, 3) if 1 <= i < 7 else range(4):
+            down0(i, c)
         for c in range(2):
             both = [
                 T0[i, h, pl.ds(16 * c, 8, stride=2), :] + T0[i, h, pl.ds(16 * c + 1, 8, stride=2), :]
                 for h in range(2)
             ]
             F1[i + 5, 8 * c + 8 : 8 * c + 16, :] = 0.125 * halves(*both)
-    for copy in first1 + late0:
+    for copy in first1:
         copy.start()
 
     for copy in first1:
@@ -462,6 +466,7 @@
         start1(q)
     for q in range(4, 14):
         relax1(B1, V1, True, q)
+    sent = []
     for i in range(4):
         for c in range(2):
             rows = pl.ds(8 * c + 8, 8)
@@ -473,17 +478,25 @@
                 left.append(F1[q, rows, :] - hp * ((A1[cls, rows, :] + BS[1]) * centre - total))
             T1[i, pl.ds(8 * c, 8), :] = left[0] + left[1]
         both = T1[i, pl.ds(0, 8, stride=2), :] + T1[i, pl.ds(1, 8, stride=2), :]
-        F2[4 * g + i, 8:16, :] = 0.125 * pair(both, 1)
+        sent.append(0.125 * pair(both, 1))
+    for i in range(2):
+        F2P[2 * g + i, 8:16, :] = jnp.where(even, sent[2 * i], sent[2 * i + 1])
     for copy in first2 + late1:
         copy.start()
 
     for copy in first2:
         copy.wait_recv()
 
-    def start2(q):
+    def start2(x):
         for c in range(3):
             rows = pl.ds(8 * c, 8)
-            B2[q + 2, rows, :] = F2[q, rows, :] * INV2[q, rows, :] * (RF2[q // 2, rows, :] * RPS[2])
+            both = F2P[x, rows, :]
+            scale = RF2[x, rows, :] * RPS[2]
+            planes = (jnp.where(even, both, roll(both, 1)), jnp.where(even, roll(both, -1), both))
+            for q in (2 * x, 2 * x + 1):
+                if c == 1:
+                    F2[q, rows, :] = planes[q % 2]
+                B2[q + 2, rows, :] = planes[q % 2] * INV2[q, rows, :] * scale
 
     def spread2(v_ref, q, row):
         rows = pl.ds(row, 8)
@@ -507,8 +520,8 @@
                 kept = (1.0 + KEEP) * centre if fresh else KEEP * centre + B2[q + 2, rows, :]
                 dst[q + 2, rows, :] = kept + INV2[q, rows, :] * total
 
-    for q in range(16):
-        start2(q)
+    for x in range(8):
+        start2(x)
     relax2(B2, V2, True)
     place = (sub >> 1) + lax.div(d, blocks)
     packed = zero
@@ -523,18 +536,29 @@
         packed = jnp.where(sub == x, jnp.sum(both, axis=0, keepdims=True), packed)
     G[pl.ds(d, 1), :, :] = (0.125 * packed)[None]
 
-    def tell(k, carry):
+    square = next((n for n in range(2, devs) if 2 * n * n == devs), 0)
+
+    def hops(k):
+        if not square:
+            return k
+        apart = (k // 2 % square, k // (2 * square))
+        return sum(min(n, square - n) for n in apart) + 0.5 * (k % 2)
+
+    for k in sorted(range(1, devs), key=hops, reverse=True):
+        if square:
+            y = lax.rem(lax.div(d, 2 * square) + k // (2 * square), square)
+            z = lax.rem(lax.rem(lax.div(d, 2), square) + k // 2 % square, square)
+            to = 2 * (square * y + z) + lax.rem(lax.rem(d, 2) + k % 2, 2)
+        else:
+            to = lax.rem(d + k, devs)
         pltpu.make_async_remote_copy(
             src_ref=G.at[d],
             dst_ref=G.at[d],
             send_sem=s3_send,
             recv_sem=s3_recv,
-            device_id=(g, lax.rem(d + k, devs)),
+            device_id=(g, to),
             device_id_type=MESH,
         ).start()
-        return carry
-
-    lax.fori_loop(1, devs, tell, 0)
 
     def wrap(k, ref):
         count = counts[k]
@@ -746,7 +770,7 @@
 
     def on_device(source, plane_layer, layer_permittivity, tile_kind, kind_fill):
         vmem = pl.BlockSpec(memory_space=pltpu.VMEM)
-        hbm = pl.BlockSpec(memory_space=pl.ANY)
+        hbm = pl.BlockSpec(memory_space=pltpu.HBM)
         tiles = devs + 2
         coarse = rows(3, tiles, 8)
         out = jax.ShapeDtypeStruct(source.shape, jnp.float32)
@@ -761,7 +785,7 @@
             rows(18, 32), rows(18, 32), rows(6, 32), rows(6, 32),
             rows(6, 32), rows(6, 32), rows(6, 32), rows(6, 32), rows(6, 48),
             rows(4, 16), rows(8, 24),
-            rows(16, 24), rows(20, 24), rows(20, 24), rows(20, 24),
+            rows(16, 24), rows(8, 24), rows(20, 24), rows(20, 24), rows(20, 24),
             rows(16, 24), rows(16, 24), rows(8, 24), rows(8, 24),
             rows(8, 24), rows(8, 24), rows(8, 24), rows(8, 24), rows(10, 40),
             rows(8, 8),

time: 42.5 us -> 42 us (0.988)
  Pallas kernels: 39 us -> 38.4 us
    pallas_call x1, Pallas kernels: 39 us -> 38.4 us  [on_device(): pl.pallas_call(functools.partial(kernel, groups, devs), out_shape=(out, o...]
where the time goes in v3:
time: 42 us; the launch traced here: 41.8 us
  Pallas kernels  38.4 us (91%)
  local copies, waits for them, and re-layouts  2.74 us (7%)
  between operations  0.65 us (2%)
    pallas_call x1, Pallas kernels, on_device(): pl.pallas_call(functools.partial(kernel, groups, devs), out_shape=(out, o...  38.4 us
    unnamed x4, local copies, waits for them, and re-layouts  2.74 us

profile of v3, /device:TPU:1, one launch (start us, length us, event | category | flops | bytes accessed | tf_op | source)
XLA Modules:
  0.0 41.8 jit_solution(10766956859562173358)
XLA Ops:
  0.6 38.4 %shard_map.68 = (f32[16,32,256]{2,1,0:T(8,128)}, f32[16,32,256]{2,1,0:T(8,128)}) custom-call(s32[2,128]{1,0:T(2,128)} %bitcast.1, s32[8,128]{1,0:T(8,128)} %kinds_hbm.1, f32[8]{0:T(128)} %permit_hbm.1, f32[16]{0:T(128)} %fill_hbm.1, f32[16,32,256]{2,1,0:T(8,128)} %source.1), custom_call_target="tpu_custom_call" | custom-call | tf_op jit(solution)/shard_map/pallas_call | solution.py:798
  39.1 0.0 copy-start
  39.1 1.9 %copy.9 = f32[16,32,256]{2,1,0:T(8,128)} copy(f32[16,32,256]{2,1,0:T(8,128)} %get-tuple-element.4) | data formatting | bytes 1048576
  41.0 0.0 copy-done
  41.0 0.8 %copy.10 = f32[16,32,256]{2,1,0:T(8,128)} copy(f32[16,32,256]{2,1,0:T(8,128)S(1)} %copy-done) | data formatting | bytes 1048576
Async XLA Ops:
  39.1 2.0 %copy-start = (f32[16,32,256]{2,1,0:T(8,128)S(1)}, f32[16,32,256]{2,1,0:T(8,128)}, u32[]{:S(2)}) copy-start(f32[16,32,256]{2,1,0:T(8,128)} %get-tuple-element.5) | copy-start | bytes 1572868
